TPU v7x, 512 devices: a whole 4x4x16 slice. The times are simulated.
512 devices in a mesh: dom: 128 (over z, y, core), rhs: 4 (over x).
Axes of the slice: x: 4, y: 4, z: 16, core: 2. Of those that a mesh axis runs over, the one named last changes fastest.
Arguments:
- elem_count: int32 [128], P('dom'), may hold values from 1 to 2, as said below
- face_count: int32 [128], P('dom'), may hold values from 4 to 9, as said below
- bound_slot: int32 [128, 2], P('dom'), may hold values from 2 to 7, as said below
- elem_face: int32 [256, 6], P('dom'), may hold values from 0 to 10, as said below
- density: float32 [256, 768], P('dom'), may hold values from 0.25 to 4
- coupling: bfloat16 [256, 768, 768], P('dom', None, 'rhs'), may hold values from -1 to 2
- ainv: bfloat16 [768, 768], replicated, may hold values from -1 to 3, as said below
- loads: bfloat16 [256, 32, 768], P('dom', 'rhs'), may hold values from -60 to 60
Outputs:
- solution: float32 [1152, 32, 128], P('dom', 'rhs')
- residual: float32 [1152, 32, 128], P('dom', 'rhs')
Inputs may be any that keep to these rules, and one draw needn't show every extreme that they name: `elem_count`: some device has 2; the live slots of a device come first. `face_count`: the live face slots of a device come first; some device has 9. `bound_slot`: entry 0 is the slot of the face the device owns at its boundary with the previous device, entry 1 that of the face it owns at its boundary with the next device; the first device's entry 0 face and the last device's entry 1 face are read by no other device. `elem_face`: the six entries of a live element are distinct; every live face slot is named by one or two live elements; dead element slots hold 0. `ainv`: symmetric.
All inputs are finite; a program needn't handle non-finite values.
Results may differ from a plain program's by a relative error of at most 0.01.
Values may be sent and summed in bfloat16 or wider, within the bound.
A program may use at most 64 MiB of HBM per device.

v0:
```python
import jax
import jax.numpy as jnp
from jax import lax
from jax.sharding import PartitionSpec as P

FSZ = 128
ITERS = 3
FCAP = 9


FULL_ACCURACY = lax.Precision.HIGHEST


def with_halo(shard, sides, width):
    for axis, dim in sides:
        count, length = (lax.axis_size(axis), shard.shape[dim])
        up = [(i, (i + 1) % count) for i in range(count - 1)]
        down = [(j, i) for i, j in up]
        last = lax.slice_in_dim(shard, length - width, length, axis=dim)
        first = lax.slice_in_dim(shard, 0, width, axis=dim)
        before = lax.ppermute(last, axis, up)
        after = lax.ppermute(first, axis, down)
        shard = jnp.concatenate([before, shard, after], axis=dim)
    return shard


def per_device(elem_count, face_count, bound_slot, elem_face, density, coupling, ainv, loads):
    elem_slots = elem_face.shape[0]
    nfaces = FCAP
    extended_size = nfaces + 2
    alive_mask = (jnp.arange(elem_slots) < elem_count[0]).astype(jnp.float32)
    scaling = lax.rsqrt(density)
    scaled = (scaling[:, :, None] * coupling.astype(jnp.float32)).astype(jnp.bfloat16)
    weighted = (scaling[:, None, :] * loads.astype(jnp.float32)).astype(jnp.bfloat16)
    forced = jnp.einsum("erf,fg->erg", weighted, ainv, preferred_element_type=jnp.float32).astype(
        jnp.bfloat16
    )
    applied = jnp.einsum("fg,egc->efc", ainv, scaled, preferred_element_type=jnp.float32).astype(
        jnp.bfloat16
    )
    right_operand = jnp.concatenate([applied, jnp.transpose(forced, (0, 2, 1))], axis=2)
    products = jnp.einsum(
        "efk,efc->ekc",
        lax.all_gather(scaled, "rhs", axis=2, tiled=True),
        right_operand,
        preferred_element_type=jnp.float32,
    )
    own_cols = scaled.shape[2]
    schur_full = lax.all_gather(products[:, :, :own_cols], "rhs", axis=2, tiled=True)
    driving = jnp.transpose(products[:, :, own_cols:], (0, 2, 1))
    schur_full = schur_full * alive_mask[:, None, None]
    driving = driving * alive_mask[:, None, None]
    schur_blocks = schur_full.reshape(elem_slots, 6, FSZ, 6, FSZ)
    choose_entries = (elem_face[:, :, None] == jnp.arange(extended_size)[None, None, :]).astype(
        jnp.float32
    )
    boundary_choose = (bound_slot[0][:, None] == jnp.arange(nfaces)[None, :]).astype(jnp.float32)

    def give_back(contribution):
        padded = with_halo(contribution[nfaces:], (("dom", 0),), 1)
        interior_part = jnp.concatenate([padded[:1], padded[3:]], axis=0)
        return contribution[:nfaces] + jnp.einsum(
            "lc,lxy->cxy", boundary_choose, interior_part, precision=FULL_ACCURACY
        )

    diagonal_pick = jnp.arange(6)
    tile_blocks = schur_blocks[:, diagonal_pick, :, diagonal_pick, :]
    tile_select = jnp.transpose(choose_entries, (1, 0, 2))
    tile_sum = jnp.einsum("kcm,kcab->mab", tile_select, tile_blocks, precision=FULL_ACCURACY)
    padded_tiles = with_halo(tile_sum[nfaces:], (("dom", 0),), 1)
    inward_tiles = jnp.concatenate([padded_tiles[:1], padded_tiles[3:]], axis=0)
    diag_blocks = tile_sum[:nfaces] + jnp.einsum(
        "ms,mab->sab", boundary_choose, inward_tiles, precision=FULL_ACCURACY
    )
    face_alive = jnp.arange(nfaces) < face_count[0]
    diag_blocks = jnp.where(
        face_alive[:, None, None], diag_blocks, jnp.eye(FSZ, dtype=jnp.float32)[None]
    )
    factor = jnp.linalg.cholesky(diag_blocks)
    identity_stack = jnp.broadcast_to(jnp.eye(FSZ, dtype=jnp.float32)[None], diag_blocks.shape)
    block_inverse = jax.scipy.linalg.cho_solve((factor, True), identity_stack)
    forcing_blocks = driving.reshape(elem_slots, driving.shape[1], 6, FSZ)
    forcing_sum = jnp.einsum(
        "doe,dwos->ews", choose_entries, forcing_blocks, precision=FULL_ACCURACY
    )
    right_side = give_back(forcing_sum)

    def precondition(vector):
        return jnp.einsum("fab,frb->fra", block_inverse, vector, precision=FULL_ACCURACY)

    def residual_dot(residual, precond_res):
        return lax.psum(jnp.sum(residual * precond_res, axis=(0, 2)), "dom")

    solution = jnp.zeros_like(right_side)
    residual = right_side
    precond_res = precondition(residual)
    search_vector = precond_res
    norm_now = residual_dot(residual, precond_res)
    for iteration in range(ITERS):
        boundary_rows = jnp.einsum(
            "ga,ahu->ghu", boundary_choose, search_vector, precision=FULL_ACCURACY
        )
        take_padded = with_halo(boundary_rows, (("dom", 0),), 1)
        enlarged_vector = jnp.concatenate([search_vector, take_padded[:1], take_padded[3:]], axis=0)
        element_local_values = jnp.einsum(
            "bsl,lae->bsae", choose_entries, enlarged_vector, precision=FULL_ACCURACY
        )
        element_out = jnp.einsum(
            "ckalb,clrb->ckra", schur_blocks, element_local_values, precision=FULL_ACCURACY
        )
        apply_contribution = jnp.einsum(
            "ckm,ckra->mra", choose_entries, element_out, precision=FULL_ACCURACY
        )
        image = give_back(apply_contribution)
        step_size = norm_now / lax.psum(jnp.sum(search_vector * image, axis=(0, 2)), "dom")
        solution = solution + step_size[None, :, None] * search_vector
        residual = residual - step_size[None, :, None] * image
        precond_res = precondition(residual)
        norm_next = residual_dot(residual, precond_res)
        search_vector = precond_res + (norm_next / norm_now)[None, :, None] * search_vector
        norm_now = norm_next
    return (solution, residual)


def solution(mesh):
    placed = (
        P("dom"),
        P("dom"),
        P("dom", None),
        P("dom", None),
        P("dom", None),
        P("dom", None, "rhs"),
        P(),
        P("dom", "rhs", None),
    )
    return jax.shard_map(
        per_device,
        mesh=mesh,
        in_specs=placed,
        out_specs=(P("dom", "rhs", None), P("dom", "rhs", None)),
        check_vma=False,
    )
```

profile of v0, /device:TPU:1, one launch (start us, length us, event | category | flops | bytes accessed | tf_op | source)
XLA Modules:
  0.0 1656.1 jit_solution(11635279389129402691)
XLA Ops:
  7.2 0.8 rsqrt.3
  8.0 2.0 multiply_convert_fusion
  10.1 1.0 fusion.7
  11.1 1.7 fusion
  12.8 43.1 %all-gather.3.cloned.1.call-done = bf16[2,768,768]{1,2,0:T(8,128)(2,1)} async-done(((bf16[2,768,192]{1,2,0:T(8,128)(2,1)}), bf16[2,768,768]{1,2,0:T(8,128)(2,1)}) %all-gather.3.cloned.1.call-update) | async-done | bytes 2359312 | tf_op jit(solution)/shard_map/all_gather | solution.py:44
  55.9 2.6 fusion.11
  58.5 1.1 slice.131
  62.7 2.7 collective-permute-start.1
  65.5 3.0 collective-permute-start
  68.5 51.6 %all-gather.5.cloned.1.call-done = f32[2,768,768]{1,2,0:T(8,128)} async-done(((f32[2,768,192]{1,2,0:T(8,128)}), f32[2,768,768]{1,2,0:T(8,128)}) %all-gather.5.cloned.1.call-update) | async-done | bytes 4718608 | tf_op jit(solution)/shard_map/all_gather | solution.py:49
  120.1 4.9 broadcast_multiply_fusion
  125.1 6.6 reshape.76
  131.6 6.0 copy.57
  137.6 3.0 gather_fusion
  140.6 1.3 convolution_bitcast_fusion
  142.0 2.7 collective-permute-start.3
  144.8 3.2 collective-permute-start.2
  149.1 0.8 fusion.21
  150.6 105.5 %custom-call.11 = f32[9,128,128]{2,1,0:T(8,128)S(1)} custom-call(f32[9,128,128]{2,1,0:T(8,128)S(1)} %fusion.19), custom_call_target="Cholesky" | custom-call | tf_op jit(solution)/shard_map/jit(cholesky)/cholesky | solution.py:79
  256.5 88.4 %custom-call.12 = f32[9,1,128,128]{2,3,1,0:T(8,128)S(1)} custom-call(f32[9,1,128,128]{3,2,1,0:T(8,128)S(1)} %select_bitcast_fusion), custom_call_target="InvertDiagBlocksLowerTriangular" | custom-call | tf_op jit(solution)/shard_map/jit(_cho_solve)/vmap()/triangular_solve | solution.py:81
  344.9 1.1 fusion.17
  346.7 1.0 fusion.55
  348.0 1.9 collective-permute-start.5
  349.9 4.5 collective-permute-start.4
  355.1 5.7 convolution_bitcast_fusion.10
  361.1 1.9 collective-permute-start.7
  363.1 4.2 collective-permute-start.6
  367.3 0.7 collective-permute-done.6
  368.4 248.7 %all-reduce = (f32[8]{0:T(128)S(1)}, f32[8]{0:T(128)S(1)}) all-reduce(f32[8]{0:T(128)S(1)} %get-tuple-element.9, f32[8]{0:T(128)S(1)} %get-tuple-element.8), channel_id=1, replica_groups=mesh['dom'=128,'rhs'=4] {'dom'}, use_global_device_ids=true, to_apply=%region_3.4 | all-reduce | flops 16 | bytes 128 | tf_op jit(solution)/shard_map/psum | solution.py:92
  617.2 1.0 fusion.53
  618.4 250.0 %psum.44 = f32[8]{0:T(128)S(1)} all-reduce(f32[8]{0:T(128)S(1)} %fusion.27), channel_id=1, replica_groups=mesh['dom'=128,'rhs'=4] {'dom'}, use_global_device_ids=true, to_apply=%region_7.8 | all-reduce | flops 8 | bytes 64 | tf_op jit(solution)/shard_map/psum | solution.py:92
  868.7 2.6 collective-permute-start.9
  871.3 3.0 collective-permute-start.8
  874.3 0.7 collective-permute-done.8
  875.2 5.7 convolution_bitcast_fusion.9
  881.3 1.9 collective-permute-start.11
  883.2 4.2 collective-permute-start.10
  887.4 0.7 collective-permute-done.10
  888.5 244.5 %psum.45 = f32[8]{0:T(128)S(1)} all-reduce(f32[8]{0:T(128)S(1)} %get-tuple-element.31), channel_id=1, replica_groups=mesh['dom'=128,'rhs'=4] {'dom'}, use_global_device_ids=true, to_apply=%region_9.10 | all-reduce | flops 8 | bytes 64 | tf_op jit(solution)/shard_map/psum | solution.py:115
  1133.1 1.0 fusion.51
  1134.3 249.0 %psum.46 = f32[8]{0:T(128)S(1)} all-reduce(f32[8]{0:T(128)S(1)} %fusion.28), channel_id=1, replica_groups=mesh['dom'=128,'rhs'=4] {'dom'}, use_global_device_ids=true, to_apply=%region_11.12 | all-reduce | flops 8 | bytes 64 | tf_op jit(solution)/shard_map/psum | solution.py:92
  1383.6 2.6 collective-permute-start.13
  1386.1 3.0 collective-permute-start.12
  1389.2 0.7 collective-permute-done.12
  1390.1 5.7 convolution_bitcast_fusion.8
  1396.1 1.9 collective-permute-start.15
  1398.1 4.2 collective-permute-start.14
  1403.4 244.5 %psum.47 = f32[8]{0:T(128)S(1)} all-reduce(f32[8]{0:T(128)S(1)} %get-tuple-element.33), channel_id=1, replica_groups=mesh['dom'=128,'rhs'=4] {'dom'}, use_global_device_ids=true, to_apply=%region_13.14 | all-reduce | flops 8 | bytes 64 | tf_op jit(solution)/shard_map/psum | solution.py:115
  (80 shorter events, 11.7 us)
Async XLA Ops:
  7.2 2.9 copy-start
  7.2 48.7 %all-gather.3.cloned.1.call-start = ((), (), s32[]{:S(2)}) async-start(), calls=%async_computation | async-start | bytes 2949120 | tf_op jit(solution)/shard_map/all_gather | solution.py:44
  10.0 110.1 %all-gather.5.cloned.1.call-start = ((), (), s32[]{:S(2)}) async-start(), calls=%async_computation.1 | async-start | bytes 5898240 | tf_op jit(solution)/shard_map/all_gather | solution.py:49
  58.5 3.9 copy-start.1
  62.7 85.2 %collective-permute-start.1 = (f32[1,8,128]{2,0,1:T(1,128)S(1)}, f32[1,8,128]{2,0,1:T(1,128)S(1)}, u32[]{:S(2)}, u32[]{:S(2)}) collective-permute-start(f32[1,8,128]{2,0,1:T(1,128)S(1)} %get-tuple-element.21), channel_id=1, source_target_pairs={{4,0},{8,4},{12,8},{16,12},{20,16},{24,20},{28,24},{32,28},{36,32}... | collective-permute-start | bytes 12296 | tf_op jit(solution)/shard_map/ppermute | solution.py:22
  65.5 82.5 %collective-permute-start = (f32[1,8,128]{2,0,1:T(1,128)S(1)}, f32[1,8,128]{2,0,1:T(1,128)S(1)}, u32[]{:S(2)}, u32[]{:S(2)}) collective-permute-start(f32[1,8,128]{2,0,1:T(1,128)S(1)} %get-tuple-element.20), channel_id=1, source_target_pairs={{0,4},{4,8},{8,12},{12,16},{16,20},{20,24},{24,28},{28,32},{32,36}... | collective-permute-start | bytes 12296 | tf_op jit(solution)/shard_map/ppermute | solution.py:21
  137.6 10.4 copy-start.4
  142.0 6.6 collective-permute-start.3
  144.8 4.3 collective-permute-start.2
  150.3 105.8 %copy-start.3 = (pred[128,128]{1,0:T(8,128)(4,1)S(1)}, pred[128,128]{1,0:T(8,128)(4,1)}, u32[]{:S(2)}) copy-start(pred[128,128]{1,0:T(8,128)(4,1)} %iota_compare_fusion) | copy-start | bytes 49156
  150.3 106.0 %copy-start.2 = (pred[128,128]{1,0:T(8,128)(4,1)S(1)}, pred[128,128]{1,0:T(8,128)(4,1)}, u32[]{:S(2)}) copy-start(pred[128,128]{1,0:T(8,128)(4,1)} %iota_compare_fusion.1) | copy-start | bytes 49156
  348.0 6.4 collective-permute-start.5
  349.9 5.0 collective-permute-start.4
  361.1 6.1 collective-permute-start.7
  363.1 4.9 collective-permute-start.6
  868.7 5.6 collective-permute-start.9
  871.3 3.7 collective-permute-start.8
  881.3 6.1 collective-permute-start.11
  883.2 4.9 collective-permute-start.10
  1383.6 5.6 collective-permute-start.13
  1386.1 3.7 collective-permute-start.12
  1396.1 6.1 collective-permute-start.15
  1398.1 4.9 collective-permute-start.14
Sparse Core Ops, SparseCore 0:
  10.1 45.7 all-gather.2
  59.8 60.3 all-gather.4
where the time goes:
time: 1680 us; the launch traced here: 1660 us
  blocking collectives  1240 us (74%)
  other arithmetic  203 us (12%)
  waiting for transfers between devices  99.4 us (6%)
  starting transfers between devices  47.6 us (3%)
  matrix products  33.3 us (2%)
  local copies, waits for them, and re-layouts  19.8 us (1%)
    psum x3, blocking collectives, residual_dot(): return lax.psum(jnp.sum(residual * precond_res, axis=(0, 2)), 'dom')  748 us
    psum x2, blocking collectives, per_device(): lax.psum(jnp.sum(search_vector * image, axis=(0, 2)), 'dom')  489 us
    another operation x4, other arithmetic, per_device(): factor = jnp.linalg.cholesky(diag_blocks)  106 us
    another operation x3, other arithmetic, per_device(): block_inverse = jax.scipy.linalg.cho_solve((factor, True), identity_stack)  89.2 us
    all_gather x1, waiting for transfers between devices, per_device(): lax.all_gather(products[:, :, :own_cols], 'rhs', axis=2, tiled=True)  51.6 us
    all_gather x1, waiting for transfers between devices, per_device(): lax.all_gather(scaled, 'rhs', axis=2, tiled=True)  43.1 us
  transfers between devices with their start and end apart: 18, of which 9 were waited for; matrix products, arithmetic and copies ran while one was open for 2% of the time, Pallas kernels for 0%

commit v1 on v0

v1 whole, which is shorter than its diff:
```python
import functools

import jax
import jax.numpy as jnp
from jax import lax
from jax.experimental import pallas as pl
from jax.experimental.pallas import tpu as pltpu
from jax.sharding import PartitionSpec as P

FSZ = 128
NF = 9
TR = 768
NR = 16
PLANE = 8
F32 = jnp.float32
BF16 = jnp.bfloat16
MESH = pl.DeviceIdType.MESH


def parts(v):
    hi = v.astype(BF16).astype(F32)
    return jnp.concatenate([hi, v - hi], axis=0).astype(BF16)


def mm(a, b):
    return jnp.dot(a, b, preferred_element_type=F32)


def face(k):
    return slice(k * FSZ, (k + 1) * FSZ)


def kernel(
    nd, npl,
    ec, fc, bs, ef, dens, cpk, loads, ainv, sol, res,
    craw, cmat, btm, sbc, lrecv, drv, dloc, dpar, dsnd, dnbr, msc, dinv,
    tvec, tnb, rvec, rnb, vbuf, vpar, vnb, vnbr, outb, pay, ra, rb,
    lsem, csend, crecv, lsend, lrecvs, dsend, drecv, tsend, trecv, vsend, vrecv,
    asend, arecv, bsend, brecv,
):
    d = lax.axis_index("dom")
    x = lax.axis_index("rhs")
    e = lax.rem(x, 2)
    h = x // 2
    oe = 1 - e
    partner = 2 * h + oe
    nxt, prv = lax.rem(d + 1, nd), lax.rem(d + nd - 1, nd)
    nz = nd // npl
    zz, jj = d // npl, lax.rem(d, npl)
    me_a = jj * 2 + e

    def dev(dd, xx):
        return {"dom": dd, "rhs": xx}

    own = pltpu.make_async_copy(cpk.at[e], craw.at[x], lsem)
    own.start()

    bar = pltpu.get_barrier_semaphore()

    def hello(dd, xx):
        pl.semaphore_signal(bar, inc=1, device_id=dev(dd, xx), device_id_type=MESH)

    for o in range(1, 4):
        hello(d, lax.rem(x + o, 4))
    for q in range(2):
        hello(nxt, 2 * h + q)
        hello(prv, 2 * h + q)

    def plane_peer(o):
        s = lax.rem(me_a + o, 2 * npl)
        return zz * npl + s // 2, 2 * h + lax.rem(s, 2), s

    def axis_peer(o):
        s = lax.rem(zz + o, nz)
        return s * npl + jj, x, s

    @pl.loop(1, 2 * npl)
    def _(o):
        dd, xx, _s = plane_peer(o)
        hello(dd, xx)

    @pl.loop(1, nz)
    def _(o):
        dd, xx, _s = axis_peer(o)
        hello(dd, xx)

    pl.semaphore_wait(bar, 3 + 4 + 2 * npl - 1 + nz - 1)

    def remote(src, dst, ssem, rsem, dd, xx):
        return pltpu.make_async_remote_copy(
            src_ref=src, dst_ref=dst, send_sem=ssem, recv_sem=rsem,
            device_id=dev(dd, xx), device_id_type=MESH,
        )

    def shard_to(o):
        xx = lax.rem(x + o, 4)
        return remote(cpk.at[lax.rem(xx, 2)], craw.at[x], csend.at[o], crecv.at[x], d, xx)

    def shard_from(s):
        return remote(cpk.at[0], craw.at[s], csend.at[0], crecv.at[s], d, partner)

    order = [lax.rem(partner - x + 4, 4), lax.rem(x - partner + 4, 4), 2]
    for o in order:
        shard_to(o).start()
    lcopy = remote(loads.at[oe], lrecv, lsend, lrecvs, d, partner)
    lcopy.start()

    scal = lax.rsqrt(dens[pl.ds(e, 1), :])
    for k in range(6):
        sbc[face(k), :] = jnp.transpose(jnp.broadcast_to(scal[:, face(k)], (FSZ, FSZ)))

    alive = (e < ec[0]).astype(F32)
    al = [(q < ec[0]).astype(F32) for q in range(2)]
    n0 = [ef[0, k] for k in range(6)]
    n1 = [ef[1, k] for k in range(6)]
    mine = [ef[e, k] for k in range(6)]
    theirs = [ef[oe, k] for k in range(6)]
    lo_slot, up_slot = bs[0, 0], bs[0, 1]
    has_prev = (d > 0).astype(F32)
    has_next = (d < nd - 1).astype(F32)

    def eq(a, b):
        return (a == b).astype(F32)

    to_next = [[eq(mine[k], up_slot) for k in range(6)], [eq(mine[k], NF + 1) for k in range(6)]]
    to_prev = [[eq(mine[k], lo_slot) for k in range(6)], [eq(mine[k], NF) for k in range(6)]]
    same = [[eq(mine[k], theirs[q]) for q in range(6)] for k in range(6)]
    from_prev = [
        [eq(mine[k], NF) * has_prev, eq(mine[k], lo_slot) * has_prev] for k in range(6)
    ]
    from_next = [
        [eq(mine[k], NF + 1) * has_next, eq(mine[k], up_slot) * has_next] for k in range(6)
    ]

    lane = lax.broadcasted_iota(jnp.int32, (TR // 2, FSZ), 1)
    amat = ainv[...]
    own.wait()
    for t in range(2):
        p = lax.rem(h + t, 2)
        if t == 0:
            shard_from(partner).wait_recv()
        else:
            shard_from(2 * p).wait_recv()
            shard_from(2 * p + 1).wait_recv()
        cols = pl.multiple_of(p * 384, 128)
        ev, od = craw.at[2 * p], craw.at[2 * p + 1]
        cmat[:, pl.ds(cols, FSZ)] = (ev[0:TR, :].astype(F32) * sbc[...]).astype(BF16)
        cmat[:, pl.ds(cols + 2 * FSZ, FSZ)] = (od[0:TR, :].astype(F32) * sbc[...]).astype(BF16)
        m0, m1 = ev[TR:, :].astype(F32), od[TR:, :].astype(F32)
        top = jnp.where(lane < 64, m0, m1)
        bot = pltpu.roll(jnp.where(lane < 64, m1, m0), 64, 1)
        half = TR // 2
        cmat[0:half, pl.ds(cols + FSZ, FSZ)] = (top * sbc[0:half, :]).astype(BF16)
        cmat[half:TR, pl.ds(cols + FSZ, FSZ)] = (bot * sbc[half:TR, :]).astype(BF16)
        for k in range(3):
            ck = cmat[:, pl.ds(cols + k * FSZ, FSZ)]
            bt = lax.dot_general(
                ck, amat, (((0,), (0,)), ((), ())), preferred_element_type=F32
            ).astype(BF16)
            btm[pl.ds(cols + k * FSZ, FSZ), :] = bt
            dk = mm(bt, ck) * alive
            dloc[3 * p + k] = 0.5 * (dk + jnp.transpose(dk))

    xl, xr = lax.rem(x + 3, 4), lax.rem(x + 1, 4)
    dcp = [
        remote(dloc.at[0:3], dpar.at[0:3], dsend.at[0], drecv.at[0], d, xl),
        remote(dloc.at[3:6], dpar.at[3:6], dsend.at[1], drecv.at[1], d, xr),
    ]
    for c in dcp:
        c.start()
    for side, table in enumerate((to_next, to_prev)):
        for s in range(2):
            acc = table[s][0] * dloc[0]
            for k in range(1, 6):
                acc += table[s][k] * dloc[k]
            dsnd[side, s * FSZ : (s + 1) * FSZ, :] = acc
        slot = up_slot if side == 0 else lo_slot
        live = (slot < fc[0]).astype(F32)
        dsnd[side, 2 * FSZ :, :] = jnp.full((8, FSZ), 1.0, F32) * live
    for side, dd in enumerate((nxt, prv)):
        for q in range(2):
            c = remote(
                dsnd.at[side], dnbr.at[side, e], dsend.at[2 + 2 * side + q],
                drecv.at[2 + 2 * side + e], dd, 2 * h + q,
            )
            c.start()
            dcp.append(c)

    def send_all(ex, t):
        tvec[ex] = t
        out = [remote(tvec.at[ex], rvec.at[ex], tsend.at[ex, 0], trecv.at[ex, 0], d, partner)]
        out[0].start()
        for side, table in enumerate((to_next, to_prev)):
            for s in range(2):
                acc = table[s][0] * t[:, face(0)]
                for k in range(1, 6):
                    acc += table[s][k] * t[:, face(k)]
                tnb[ex, side, s] = acc
            dd = (nxt, prv)[side]
            for q in range(2):
                c = remote(
                    tnb.at[ex, side], rnb.at[ex, side, e], tsend.at[ex, 1 + 2 * side + q],
                    trecv.at[ex, 1 + 2 * side + e], dd, 2 * h + q,
                )
                c.start()
                out.append(c)
        return out

    def assemble(ex, t, cps):
        for c in cps:
            c.wait_send()
        remote(tvec.at[ex], rvec.at[ex], tsend.at[ex, 0], trecv.at[ex, 0], d, partner).wait_recv()
        for side in range(2):
            for q in range(2):
                remote(
                    tnb.at[ex, side], rnb.at[ex, side, q], tsend.at[ex, 0],
                    trecv.at[ex, 1 + 2 * side + q], d, partner,
                ).wait_recv()
        pv = [rnb[ex, 0, 0, s] + rnb[ex, 0, 1, s] for s in range(2)]
        nv = [rnb[ex, 1, 0, s] + rnb[ex, 1, 1, s] for s in range(2)]
        other = [rvec[ex, :, face(q)] for q in range(6)]
        cols = []
        for k in range(6):
            acc = t[:, face(k)]
            for q in range(6):
                acc += same[k][q] * other[q]
            acc += from_prev[k][0] * pv[0] + from_prev[k][1] * pv[1]
            acc += from_next[k][0] * nv[0] + from_next[k][1] * nv[1]
            cols.append(acc)
        return jnp.concatenate(cols, axis=1)

    lcopy.wait()
    srow = scal
    wgt = [
        (loads[e].astype(F32) * srow).astype(BF16).astype(F32),
        (lrecv[...].astype(F32) * srow).astype(BF16).astype(F32),
    ]
    low = e == 0
    weighted = jnp.concatenate(
        [jnp.where(low, wgt[0], wgt[1]), jnp.where(low, wgt[1], wgt[0])], axis=0
    ).astype(BF16)
    forced = mm(weighted, amat).astype(BF16)
    rloc = mm(forced, cmat[...]) * alive
    drv[...] = rloc
    rcp = send_all(0, rloc)

    for c in dcp:
        c.wait_send()
    remote(dloc.at[0:3], dpar.at[0:3], dsend.at[0], drecv.at[0], d, partner).wait_recv()
    remote(dloc.at[3:6], dpar.at[3:6], dsend.at[0], drecv.at[1], d, partner).wait_recv()
    for side in range(2):
        for q in range(2):
            remote(
                dsnd.at[side], dnbr.at[side, q], dsend.at[0], drecv.at[2 + 2 * side + q], d, partner
            ).wait_recv()
    row = lax.broadcasted_iota(jnp.int32, (FSZ, FSZ), 0)
    col = lax.broadcasted_iota(jnp.int32, (FSZ, FSZ), 1)
    eye = (row == col).astype(F32)
    srows, scols = [], []
    for k in range(6):
        acc = dloc[k]
        for q in range(6):
            acc += same[k][q] * dpar[q]
        for s in range(2):
            at = slice(s * FSZ, (s + 1) * FSZ)
            acc += from_prev[k][s] * (dnbr[0, 0, at, :] + dnbr[0, 1, at, :])
            acc += from_next[k][s] * (dnbr[1, 0, at, :] + dnbr[1, 1, at, :])
        flag = jnp.full((1, FSZ), 1.0, F32) * (mine[k] < fc[0]).astype(F32)
        flag = jnp.where(mine[k] == NF, dnbr[0, 0, 2 * FSZ : 2 * FSZ + 1, :], flag)
        flag = jnp.where(mine[k] == NF + 1, dnbr[1, 0, 2 * FSZ : 2 * FSZ + 1, :], flag)
        acc = jnp.where(flag * alive > 0.5, acc, eye)
        diag = acc * eye
        srow_k = lax.rsqrt(jnp.sum(diag, axis=0, keepdims=True))
        scol_k = lax.rsqrt(jnp.sum(diag, axis=1, keepdims=True))
        srows.append(srow_k)
        scols.append(scol_k)
        msc[k] = acc * srow_k * scol_k

    sub8 = lax.broadcasted_iota(jnp.int32, (8, FSZ), 0)
    lane8 = lax.broadcasted_iota(jnp.int32, (8, FSZ), 1)
    diag8 = (sub8 == lane8).astype(F32)

    def split3(v):
        a1 = v.astype(BF16).astype(F32)
        a2 = (v - a1).astype(BF16).astype(F32)
        return a1, a2, v - a1 - a2

    def sweep(jb, carry):
        base = pl.multiple_of(jb * 8, 8)
        shift = lax.rem(FSZ - base, FSZ)
        panels = [pltpu.roll(msc[k, pl.ds(base, 8), :], shift, 1) for k in range(6)]
        inv = list(panels)
        for i in range(8):
            for k in range(6):
                r = inv[k]
                cb = jnp.broadcast_to(r[:, i : i + 1], (8, FSZ))
                pinv = 1.0 / jnp.broadcast_to(cb[i : i + 1, :], (8, FSZ))
                rb_ = jnp.broadcast_to(r[i : i + 1, :], (8, FSZ))
                rn = jnp.where(lane8 == i, 1.0, rb_) * pinv
                inv[k] = jnp.where(sub8 == i, rn, jnp.where(lane8 == i, 0.0, r) - cb * rn)
        for k in range(6):
            xm = pltpu.roll(panels[k] - diag8, base, 1)
            ym = pltpu.roll(jnp.where(lane8 < 8, diag8 - inv[k], inv[k]), base, 1)
            x1, x2, x3 = split3(xm)
            y1, y2, y3 = split3(ym)
            xs = jnp.concatenate([x1, x1, x2, x2, x1, x3], axis=0).astype(BF16)
            ys = jnp.concatenate([y1, y2, y1, y2, y3, y1], axis=0).astype(BF16)
            upd = lax.dot_general(xs, ys, (((0,), (0,)), ((), ())), preferred_element_type=F32)
            msc[k] = msc[k] - upd
            rows = jnp.where(lane8 < 8, -inv[k], inv[k])
            msc[k, pl.ds(base, 8), :] = pltpu.roll(rows, base, 1)
        return carry

    lax.fori_loop(0, FSZ // 8, sweep, 0)
    for k in range(6):
        di = -(msc[k] * srows[k] * scols[k])
        hi = di.astype(BF16)
        dinv[k, :, 0:FSZ] = hi
        dinv[k, :, FSZ:] = (di - hi.astype(F32)).astype(BF16)

    def precondition(v):
        out = []
        for k in range(6):
            y = mm(parts(v[:, face(k)]), dinv[k])
            y = y[:NR] + y[NR:]
            out.append(y[:, :FSZ] + y[:, FSZ:])
        return jnp.concatenate(out, axis=1)

    def apply_s(v):
        u = mm(parts(v), btm[...])
        u = u[:NR] + u[NR:]
        t = mm(parts(u), cmat[...])
        return (t[:NR] + t[NR:]) * alive

    r0 = assemble(0, rloc, rcp)
    vbuf[3] = r0
    w = precondition(r0)
    vbuf[0] = w
    for i in range(3):
        t = apply_s(w)
        cps = send_all(1 + i, t)
        if i < 2:
            full = assemble(1 + i, t, cps)
            vbuf[4 + i] = full
            w = precondition(full) - w
            vbuf[1 + i] = w

    def fold(v):
        acc = v[:, face(0)]
        for k in range(1, 6):
            acc += v[:, face(k)]
        return acc

    prods = []
    for i in range(3):
        wi = vbuf[i]
        for j in range(3):
            prods.append(fold(wi * tvec[1 + j]))
        prods.append(fold(wi * drv[...]))
    pads = [jnp.zeros((NR, FSZ), F32)] * 4
    for c in range(2):
        stack = jnp.concatenate((prods + pads)[8 * c : 8 * c + 8], axis=0)
        pay[0, c : c + 1, :] = jnp.sum(jnp.transpose(stack), axis=0, keepdims=True)
    ra[me_a] = pay[0]

    def plane_send(o):
        dd, xx, s = plane_peer(o)
        return remote(pay.at[0], ra.at[me_a], asend.at[s], arecv.at[me_a], dd, xx)

    def plane_from(o):
        _dd, _xx, s = plane_peer(o)
        return remote(pay.at[0], ra.at[s], asend.at[s], arecv.at[s], d, partner)

    def axis_send(o):
        dd, xx, s = axis_peer(o)
        return remote(pay.at[1], rb.at[zz], bsend.at[s], brecv.at[zz], dd, xx)

    def axis_from(o):
        _dd, _xx, s = axis_peer(o)
        return remote(pay.at[1], rb.at[s], bsend.at[s], brecv.at[s], d, partner)

    @pl.loop(1, 2 * npl)
    def _(o):
        plane_send(o).start()

    @pl.loop(1, 2 * npl)
    def _(o):
        plane_from(o).wait_recv()

    tot = ra[0]
    for s in range(1, 2 * npl):
        tot = tot + ra[s]
    pay[1] = tot
    rb[zz] = tot

    @pl.loop(1, nz)
    def _(o):
        axis_send(o).start()

    vbuf[6] = assemble(3, t, cps)
    m0 = [sum(eq(n0[k], f) for k in range(6)) * al[0] for f in range(NF + 2)]
    m1 = [sum(eq(n1[k], f) for k in range(6)) * al[1] for f in range(NF + 2)]
    mine_w = [jnp.where(e == 0, al[0], al[1] * (1.0 - m0[f])) for f in range(NF + 2)]
    their_w = [jnp.where(e == 1, al[0], al[1] * (1.0 - m0[f])) for f in range(NF + 2)]
    for side, name in enumerate((NF + 1, NF)):
        for v in range(7):
            acc = jnp.zeros((NR, FSZ), F32)
            for k in range(6):
                acc += (eq(mine[k], name) * mine_w[name]) * vbuf[v, :, face(k)]
            vnb[side, v] = acc
    vcp = [
        remote(
            vbuf.at[:, pl.ds(pl.multiple_of(8 * oe, 8), 8), :], vpar, vsend.at[0], vrecv.at[0],
            d, partner,
        )
    ]
    for side, dd in enumerate((nxt, prv)):
        for q in range(2):
            vcp.append(
                remote(
                    vnb.at[side, :, 8 * q : 8 * q + 8, :], vnbr.at[side, e],
                    vsend.at[1 + 2 * side + q], vrecv.at[1 + 2 * side + e], dd, 2 * h + q,
                )
            )
    for c in vcp:
        c.start()
    for c in vcp:
        c.wait_send()
    remote(vpar, vpar, vsend.at[0], vrecv.at[0], d, partner).wait_recv()
    for side in range(2):
        for q in range(2):
            remote(
                vnb.at[side, :, 0:8, :], vnbr.at[side, q], vsend.at[0],
                vrecv.at[1 + 2 * side + q], d, partner,
            ).wait_recv()
    rows = pl.ds(pl.multiple_of(8 * e, 8), 8)
    for f in range(NF):
        free = 1.0 - jnp.maximum(m0[f], m1[f])
        wp = free * eq(lo_slot, f) * has_prev
        wn = free * eq(up_slot, f) * has_next
        for v in range(7):
            acc = wp * (vnbr[0, 0, v] + vnbr[0, 1, v]) + wn * (vnbr[1, 0, v] + vnbr[1, 1, v])
            for k in range(6):
                acc += (eq(mine[k], f) * mine_w[f]) * vbuf[v, rows, face(k)]
                acc += (eq(theirs[k], f) * their_w[f]) * vpar[v, :, face(k)]
            outb[v, f] = acc

    @pl.loop(1, 2 * npl)
    def _(o):
        plane_send(o).wait_send()

    @pl.loop(1, nz)
    def _(o):
        axis_from(o).wait_recv()

    @pl.loop(1, nz)
    def _(o):
        axis_send(o).wait_send()

    for o in order:
        shard_to(o).wait_send()
    tot = rb[0]
    for s in range(1, nz):
        tot = tot + rb[s]

    def pick(q):
        r = jnp.broadcast_to(tot[q // 8 : q // 8 + 1, :], (8, FSZ))
        at = (q % 8) * NR + 8 * e
        return jnp.sum(jnp.where(lane8 == sub8 + at, r, 0.0), axis=1, keepdims=True)

    g = [[pick(4 * i + j) for j in range(3)] for i in range(3)]
    gr = [pick(4 * i + 3) for i in range(3)]

    zero = jnp.zeros((8, 1), F32)
    pi = [zero + 1.0, zero, zero]
    rho = [zero, zero, zero]
    xc = [zero, zero, zero]
    rz = gr[0]
    for it in range(3):
        psp = zero
        for i in range(it + 1):
            for j in range(it + 1):
                psp += pi[i] * pi[j] * g[i][j]
        alpha = rz / psp
        xc = [xc[i] + alpha * pi[i] for i in range(3)]
        rho = [rho[i] - alpha * pi[i] for i in range(3)]
        if it == 2:
            break
        zc = [1.0 + rho[0], rho[0] + rho[1], rho[1] + rho[2]]
        new = zero
        for i in range(it + 2):
            s = gr[i]
            for j in range(it + 1):
                s += rho[j] * g[i][j]
            new += zc[i] * s
        beta = new / rz
        pi = [zc[i] + beta * pi[i] for i in range(3)]
        rz = new
    xb = [jnp.broadcast_to(c, (8, FSZ)) for c in xc]
    rbc = [jnp.broadcast_to(c, (8, FSZ)) for c in rho]
    for f in range(NF):
        sol[f] = xb[0] * outb[0, f] + xb[1] * outb[1, f] + xb[2] * outb[2, f]
        res[f] = outb[3, f] + rbc[0] * outb[4, f] + rbc[1] * outb[5, f] + rbc[2] * outb[6, f]


def per_device(nd, npl, elem_count, face_count, bound_slot, elem_face, density, coupling, ainv, loads):
    odd = lax.rem(lax.axis_index("rhs"), 2) == 1
    main = jnp.where(odd, coupling[:, :, 64:], coupling[:, :, :128])
    mid = jnp.where(odd, coupling[:, :, :64], coupling[:, :, 128:])
    a, b = mid[:, : TR // 2], mid[:, TR // 2 :]
    mid = jnp.where(odd, jnp.concatenate([b, a], axis=2), jnp.concatenate([a, b], axis=2))
    packed = jnp.concatenate([main, mid], axis=1)

    smem = pl.BlockSpec(memory_space=pltpu.SMEM)
    vmem = pl.BlockSpec(memory_space=pltpu.VMEM)
    hbm = pl.BlockSpec(memory_space=pl.ANY)
    dma = pltpu.SemaphoreType.DMA
    nz = nd // npl
    out = jax.ShapeDtypeStruct((NF, 8, FSZ), F32)
    vm = pltpu.VMEM
    return pl.pallas_call(
        functools.partial(kernel, nd, npl),
        out_shape=(out, out),
        in_specs=[smem, smem, smem, smem, vmem, hbm, vmem, vmem],
        out_specs=(vmem, vmem),
        scratch_shapes=[
            vm((4, 1152, FSZ), BF16),
            vm((TR, TR), BF16),
            vm((TR, TR), BF16),
            vm((TR, FSZ), F32),
            vm((8, TR), BF16),
            vm((NR, TR), F32),
            vm((6, FSZ, FSZ), F32),
            vm((6, FSZ, FSZ), F32),
            vm((2, 2 * FSZ + 8, FSZ), F32),
            vm((2, 2, 2 * FSZ + 8, FSZ), F32),
            vm((6, FSZ, FSZ), F32),
            vm((6, FSZ, 2 * FSZ), BF16),
            vm((4, NR, TR), F32),
            vm((4, 2, 2, NR, FSZ), F32),
            vm((4, NR, TR), F32),
            vm((4, 2, 2, 2, NR, FSZ), F32),
            vm((7, NR, TR), F32),
            vm((7, 8, TR), F32),
            vm((2, 7, NR, FSZ), F32),
            vm((2, 2, 7, 8, FSZ), F32),
            vm((7, NF, 8, FSZ), F32),
            vm((2, 2, FSZ), F32),
            vm((2 * npl, 2, FSZ), F32),
            vm((nz, 2, FSZ), F32),
            dma, dma((4,)), dma((4,)), dma, dma, dma((6,)), dma((6,)),
            dma((4, 5)), dma((4, 5)), dma((5,)), dma((5,)),
            dma((2 * npl,)), dma((2 * npl,)), dma((nz,)), dma((nz,)),
        ],
        compiler_params=pltpu.CompilerParams(
            collective_id=0, has_side_effects=True, vmem_limit_bytes=48 * 1024 * 1024
        ),
        name="condense_cg",
    )(elem_count, face_count, bound_slot, elem_face, density, packed, loads, ainv)


def solution(mesh):
    placed = (
        P("dom"),
        P("dom"),
        P("dom", None),
        P("dom", None),
        P("dom", None),
        P("dom", None, "rhs"),
        P(),
        P("dom", "rhs", None),
    )
    nd = mesh.shape["dom"]
    npl = min(PLANE, nd // 2)
    return jax.shard_map(
        functools.partial(per_device, nd, npl),
        mesh=mesh,
        in_specs=placed,
        out_specs=(P("dom", "rhs", None), P("dom", "rhs", None)),
        check_vma=False,
    )
```

time: 1680 us -> 97 us (0.06); the launches traced: 1660 us -> 96.8 us
  blocking collectives: 1240 us -> 0 us
  other arithmetic: 203 us -> 0.35 us
  waiting for transfers between devices: 99.4 us -> 0 us
  Pallas kernels: 0 us -> 90.3 us
  starting transfers between devices: 47.6 us -> 0 us
  matrix products: 33.3 us -> 0 us
    psum x5 -> x0, blocking collectives: 1240 us -> none  [the longest x3 748 us: residual_dot(): return lax.psum(jnp.sum(residual * precond_res, axis=(0, 2)), 'dom')]
    another operation x7 -> x0, other arithmetic: 195 us -> none  [the longest x4 106 us: per_device(): factor = jnp.linalg.cholesky(diag_blocks)]
    all_gather x2 -> x0, waiting for transfers between devices: 94.7 us -> none  [the longest x1 51.6 us: per_device(): lax.all_gather(products[:, :, :own_cols], 'rhs', axis=2, tiled=True)]
    pallas_call x0 -> x1, Pallas kernels: none -> 90.3 us  [per_device(): pl.pallas_call(functools.partial(kernel, nd, npl), out_shape=(out, out),...]
    ppermute x16 -> x0, starting transfers between devices: 47.6 us -> none  [the longest x8 29.3 us: with_halo(): before = lax.ppermute(last, axis, up)]
    dot_general x25 -> x0, matrix products: 31.5 us -> none  [the longest x3 17 us: per_device(): jnp.einsum('ckalb,clrb->ckra', schur_blocks, element_local_values, precis...]
  transfers between devices with their start and end apart: 18 -> 0, of which waited for: 9 -> 0; matrix products, arithmetic and copies ran while one was open for 2% -> 0% of each run, Pallas kernels for 0% -> 0%
where the time goes in v1:
time: 97 us; the launch traced here: 96.8 us
  Pallas kernels  90.3 us (93%)
  local copies, waits for them, and re-layouts  4.04 us (4%)
  between operations  2.17 us (2%)
    pallas_call x1, Pallas kernels, per_device(): pl.pallas_call(functools.partial(kernel, nd, npl), out_shape=(out, out),...  90.3 us
    unnamed x18, local copies, waits for them, and re-layouts  2.9 us

profile of v1, /device:TPU:1, one launch (start us, length us, event | category | flops | bytes accessed | tf_op | source)
XLA Modules:
  0.0 96.8 jit_solution(5182129736905675150)
XLA Ops:
  0.6 1.1 %fusion.1 = (bf16[2,768,64]{1,2,0:T(8,128)(2,1)S(1)}, bf16[2,768,64]{1,2,0:T(8,128)(2,1)S(1)}) fusion(bf16[2,768,192]{1,2,0:T(8,128)(2,1)} %param.13), kind=kLoop, calls=%fused_computation.5 | loop fusion | bytes 786432 | tf_op jit(solution)/shard_map/slice | solution.py:509
  1.7 0.2 copy.16
  1.9 0.2 copy.17
  2.2 0.0 copy-start.5
  2.3 0.2 maximum_select_fusion
  2.5 0.7 copy-done.5
  3.2 0.1 fusion
  3.3 0.2 copy.14
  3.5 0.2 copy.15
  3.7 0.0 copy-start
  3.7 0.0 copy-start.1
  3.8 0.0 copy-start.2
  3.8 0.0 copy-start.3
  3.8 0.0 copy-start.4
  5.3 0.0 copy-done
  5.3 0.0 copy-done.1
  5.3 0.0 copy-done.2
  5.3 0.0 copy-done.3
  5.3 0.0 copy-done.4
  5.3 90.3 %condense_cg.1 = (f32[9,8,128]{2,1,0:T(8,128)S(1)}, f32[9,8,128]{2,1,0:T(8,128)S(1)}) custom-call(s32[1]{0:T(128)S(6)} %copy.20.ec, s32[1]{0:T(128)S(6)} %copy.21.fc, s32[1,2]{1,0:T(1,128)S(1)} %copy-done.4, s32[2,6]{1,0:T(2,128)S(1)} %copy-done.3, f32[2,768]{1,0:T(2,128)S(1)} %copy-done.2, bf16[2,1152,128]{2,1,0:T(8,128)(2,1)S(1)} %pad_maximum_fusion.cpk, ...), custom_call_target="tpu_custom_call" | custom-call | tf_op jit(solution)/shard_map/condense_cg/pallas_call | solution.py:521
  95.6 0.6 copy.22
  96.2 0.6 copy.23
  (4 shorter events, 0.2 us)
Async XLA Ops:
  2.2 1.1 %copy-start.5 = (bf16[2,768,192]{1,2,0:T(8,128)(2,1)S(1)}, bf16[2,768,192]{1,2,0:T(8,128)(2,1)}, u32[]{:S(2)}) copy-start(bf16[2,768,192]{1,2,0:T(8,128)(2,1)} %param.13) | copy-start | bytes 1769476
  3.7 1.5 %copy-start = (bf16[768,768]{1,0:T(8,128)(2,1)S(1)}, bf16[768,768]{1,0:T(8,128)(2,1)}, u32[]{:S(2)}) copy-start(bf16[768,768]{1,0:T(8,128)(2,1)} %ainv.1) | copy-start | bytes 3538948
  3.7 1.5 %copy-start.1 = (bf16[2,8,768]{2,1,0:T(8,128)(2,1)S(1)}, bf16[2,8,768]{2,1,0:T(8,128)(2,1)}, u32[]{:S(2)}) copy-start(bf16[2,8,768]{2,1,0:T(8,128)(2,1)} %loads.1) | copy-start | bytes 73732
  3.8 1.5 %copy-start.2 = (f32[2,768]{1,0:T(2,128)S(1)}, f32[2,768]{1,0:T(2,128)}, u32[]{:S(2)}) copy-start(f32[2,768]{1,0:T(2,128)} %dens.1) | copy-start | bytes 18436
  3.8 1.5 %copy-start.3 = (s32[2,6]{1,0:T(2,128)S(1)}, s32[2,6]{1,0:T(2,128)}, u32[]{:S(2)}) copy-start(s32[2,6]{1,0:T(2,128)} %ef.1) | copy-start | bytes 148
  3.8 1.5 %copy-start.4 = (s32[1,2]{1,0:T(1,128)S(1)}, s32[1,2]{1,0:T(1,128)}, u32[]{:S(2)}) copy-start(s32[1,2]{1,0:T(1,128)} %bs.1) | copy-start | bytes 28

commit v2 on v1

--- a/solution.py
+++ b/solution.py
@@ -12,6 +12,8 @@
 TR = 768
 NR = 16
 PLANE = 8
+PK = 72
+BL = 16
 F32 = jnp.float32
 BF16 = jnp.bfloat16
 MESH = pl.DeviceIdType.MESH
@@ -32,10 +34,10 @@
 
 def kernel(
     nd, npl,
-    ec, fc, bs, ef, dens, cpk, loads, ainv, sol, res,
-    craw, cmat, btm, sbc, lrecv, drv, dloc, dpar, dsnd, dnbr, msc, dinv,
+    ec, fc, bs, ef, dens, coup, loads, ainv, sol, res,
+    cin, cpk, amt, craw, cmat, btm, sbc, lrecv, drv, dloc, dpar, dsnd, dnbr, msc, wrow, zrow, dinv,
     tvec, tnb, rvec, rnb, vbuf, vpar, vnb, vnbr, outb, pay, ra, rb,
-    lsem, csend, crecv, lsend, lrecvs, dsend, drecv, tsend, trecv, vsend, vrecv,
+    near, lsem, csend, crecv, lsend, lrecvs, dsend, drecv, tsend, trecv, vsend, vrecv,
     asend, arecv, bsend, brecv,
 ):
     d = lax.axis_index("dom")
@@ -52,8 +54,13 @@
     def dev(dd, xx):
         return {"dom": dd, "rhs": xx}
 
-    own = pltpu.make_async_copy(cpk.at[e], craw.at[x], lsem)
-    own.start()
+    loc = [
+        pltpu.make_async_copy(coup.at[oe], cin.at[0], lsem.at[0]),
+        pltpu.make_async_copy(coup.at[e], cin.at[1], lsem.at[1]),
+        pltpu.make_async_copy(ainv, amt, lsem.at[2]),
+    ]
+    for c in loc:
+        c.start()
 
     bar = pltpu.get_barrier_semaphore()
 
@@ -79,12 +86,34 @@
         dd, xx, _s = plane_peer(o)
         hello(dd, xx)
 
-    @pl.loop(1, nz)
-    def _(o):
-        dd, xx, _s = axis_peer(o)
-        hello(dd, xx)
-
-    pl.semaphore_wait(bar, 3 + 4 + 2 * npl - 1 + nz - 1)
+    above, below = lax.rem(zz + 1, nz) * npl + jj, lax.rem(zz + nz - 1, nz) * npl + jj
+    hello(above, x)
+    hello(below, x)
+
+    odd = e
+    src = lax.broadcasted_iota(jnp.int32, (192, FSZ), 0)
+    dst = lax.broadcasted_iota(jnp.int32, (192, FSZ), 1)
+    first_mid = 128 * (1 - odd)
+
+    p_main = (src == dst + 64 * odd).astype(F32).astype(BF16)
+    is_mid = (src >= first_mid) & (src < first_mid + 64)
+    p_low = (is_mid & (src - first_mid == dst)).astype(F32)
+    p_high = (is_mid & (src - first_mid + 64 == dst)).astype(F32)
+    o32 = odd.astype(F32)
+    p_top = (p_low * (1.0 - o32) + p_high * o32).astype(BF16)
+    p_bot = (p_high * (1.0 - o32) + p_low * o32).astype(BF16)
+
+    def pack(raw, out):
+        out[0:TR, :] = mm(raw[...], p_main).astype(BF16)
+        mid = mm(raw[0 : TR // 2, :], p_top) + mm(raw[TR // 2 :, :], p_bot)
+        out[TR:, :] = mid.astype(BF16)
+
+    loc[0].wait()
+    pack(cin.at[0], cpk)
+    loc[1].wait()
+    pack(cin.at[1], craw.at[x])
+
+    pl.semaphore_wait(bar, 3 + 4 + 2 * npl - 1 + 2)
 
     def remote(src, dst, ssem, rsem, dd, xx):
         return pltpu.make_async_remote_copy(
@@ -92,18 +121,26 @@
             device_id=dev(dd, xx), device_id_type=MESH,
         )
 
-    def shard_to(o):
-        xx = lax.rem(x + o, 4)
-        return remote(cpk.at[lax.rem(xx, 2)], craw.at[x], csend.at[o], crecv.at[x], d, xx)
+    far = lax.rem(x + 2, 4)
+    shards = [
+        remote(cpk, craw.at[x], csend.at[0], crecv.at[x], d, partner),
+        remote(craw.at[x], craw.at[x], csend.at[2], crecv.at[x], d, far),
+        remote(cpk, craw.at[x], csend.at[1], crecv.at[x], d, lax.rem(partner + 2, 4)),
+    ]
 
     def shard_from(s):
-        return remote(cpk.at[0], craw.at[s], csend.at[0], crecv.at[s], d, partner)
-
-    order = [lax.rem(partner - x + 4, 4), lax.rem(x - partner + 4, 4), 2]
-    for o in order:
-        shard_to(o).start()
+        return remote(cpk, craw.at[s], csend.at[0], crecv.at[s], d, partner)
+
+    for c in shards:
+        c.start()
     lcopy = remote(loads.at[oe], lrecv, lsend, lrecvs, d, partner)
     lcopy.start()
+
+    for _r in range(nz // 2 - 1):
+        pl.semaphore_signal(near.at[0], inc=1, device_id=dev(above, x), device_id_type=MESH)
+        pl.semaphore_signal(near.at[1], inc=1, device_id=dev(below, x), device_id_type=MESH)
+        pl.semaphore_wait(near.at[0], 1)
+        pl.semaphore_wait(near.at[1], 1)
 
     scal = lax.rsqrt(dens[pl.ds(e, 1), :])
     for k in range(6):
@@ -133,8 +170,10 @@
     ]
 
     lane = lax.broadcasted_iota(jnp.int32, (TR // 2, FSZ), 1)
-    amat = ainv[...]
-    own.wait()
+    row64 = lax.broadcasted_iota(jnp.int32, (64, FSZ), 0)
+    lane64 = lax.broadcasted_iota(jnp.int32, (64, FSZ), 1)
+    loc[2].wait()
+    amat = amt[...]
     for t in range(2):
         p = lax.rem(h + t, 2)
         if t == 0:
@@ -158,8 +197,12 @@
                 ck, amat, (((0,), (0,)), ((), ())), preferred_element_type=F32
             ).astype(BF16)
             btm[pl.ds(cols + k * FSZ, FSZ), :] = bt
-            dk = mm(bt, ck) * alive
-            dloc[3 * p + k] = 0.5 * (dk + jnp.transpose(dk))
+            dk = mm(bt, ck) * (0.5 * alive)
+            dk = dk + jnp.transpose(dk)
+            lower = pltpu.roll(dk[64:, :], 64, 1)
+            dloc[3 * p + k, 0:64, :] = jnp.where((lane64 < 64) & (lane64 < row64), lower, dk[:64, :])
+            tail = jnp.sum(jnp.where(lane64 == row64 + 64, dk[64:, :], 0.0), axis=0, keepdims=True)
+            dloc[3 * p + k, 64:, :] = jnp.broadcast_to(tail, (8, FSZ))
 
     xl, xr = lax.rem(x + 3, 4), lax.rem(x + 1, 4)
     dcp = [
@@ -173,10 +216,10 @@
             acc = table[s][0] * dloc[0]
             for k in range(1, 6):
                 acc += table[s][k] * dloc[k]
-            dsnd[side, s * FSZ : (s + 1) * FSZ, :] = acc
+            dsnd[side, s * PK : (s + 1) * PK, :] = acc
         slot = up_slot if side == 0 else lo_slot
         live = (slot < fc[0]).astype(F32)
-        dsnd[side, 2 * FSZ :, :] = jnp.full((8, FSZ), 1.0, F32) * live
+        dsnd[side, 2 * PK :, :] = jnp.full((8, FSZ), 1.0, F32) * live
     for side, dd in enumerate((nxt, prv)):
         for q in range(2):
             c = remote(
@@ -262,58 +305,99 @@
         for q in range(6):
             acc += same[k][q] * dpar[q]
         for s in range(2):
-            at = slice(s * FSZ, (s + 1) * FSZ)
+            at = slice(s * PK, (s + 1) * PK)
             acc += from_prev[k][s] * (dnbr[0, 0, at, :] + dnbr[0, 1, at, :])
             acc += from_next[k][s] * (dnbr[1, 0, at, :] + dnbr[1, 1, at, :])
         flag = jnp.full((1, FSZ), 1.0, F32) * (mine[k] < fc[0]).astype(F32)
-        flag = jnp.where(mine[k] == NF, dnbr[0, 0, 2 * FSZ : 2 * FSZ + 1, :], flag)
-        flag = jnp.where(mine[k] == NF + 1, dnbr[1, 0, 2 * FSZ : 2 * FSZ + 1, :], flag)
+        flag = jnp.where(mine[k] == NF, dnbr[0, 0, 2 * PK : 2 * PK + 1, :], flag)
+        flag = jnp.where(mine[k] == NF + 1, dnbr[1, 0, 2 * PK : 2 * PK + 1, :], flag)
+        body, tail = acc[:64, :], acc[64:65, :]
+        keep = jnp.where(lane64 == row64, 0.5, 1.0)
+        up = jnp.where(lane64 >= row64, body * keep, 0.0)
+        dn = pltpu.roll(jnp.where(lane64 < row64, body, 0.0), 64, 1)
+        dn = dn + jnp.where(lane64 == row64 + 64, 0.5 * tail, 0.0)
+        half = jnp.concatenate([up, dn], axis=0)
+        acc = half + jnp.transpose(half)
         acc = jnp.where(flag * alive > 0.5, acc, eye)
         diag = acc * eye
         srow_k = lax.rsqrt(jnp.sum(diag, axis=0, keepdims=True))
         scol_k = lax.rsqrt(jnp.sum(diag, axis=1, keepdims=True))
         srows.append(srow_k)
         scols.append(scol_k)
-        msc[k] = acc * srow_k * scol_k
-
+        msc[k * FSZ : (k + 1) * FSZ, :] = acc * srow_k * scol_k
+
+    msc[6 * FSZ : 7 * FSZ, :] = eye
+    msc[7 * FSZ :, :] = eye
     sub8 = lax.broadcasted_iota(jnp.int32, (8, FSZ), 0)
     lane8 = lax.broadcasted_iota(jnp.int32, (8, FSZ), 1)
-    diag8 = (sub8 == lane8).astype(F32)
-
-    def split3(v):
-        a1 = v.astype(BF16).astype(F32)
-        a2 = (v - a1).astype(BF16).astype(F32)
-        return a1, a2, v - a1 - a2
-
-    def sweep(jb, carry):
-        base = pl.multiple_of(jb * 8, 8)
-        shift = lax.rem(FSZ - base, FSZ)
-        panels = [pltpu.roll(msc[k, pl.ds(base, 8), :], shift, 1) for k in range(6)]
-        inv = list(panels)
+    laneb = lax.broadcasted_iota(jnp.int32, (BL, FSZ), 1)
+    rowb = lax.broadcasted_iota(jnp.int32, (BL, FSZ), 0)
+
+    def at_lane(r, i):
+        return jnp.broadcast_to(r[:, i : i + 1], (8, FSZ))
+
+    def invert8(p):
+        p = dict(p)
+
+        def key(a, b):
+            return (a, b) if a <= b else (b, a)
+
         for i in range(8):
-            for k in range(6):
-                r = inv[k]
-                cb = jnp.broadcast_to(r[:, i : i + 1], (8, FSZ))
-                pinv = 1.0 / jnp.broadcast_to(cb[i : i + 1, :], (8, FSZ))
-                rb_ = jnp.broadcast_to(r[i : i + 1, :], (8, FSZ))
-                rn = jnp.where(lane8 == i, 1.0, rb_) * pinv
-                inv[k] = jnp.where(sub8 == i, rn, jnp.where(lane8 == i, 0.0, r) - cb * rn)
+            dinv_i = 1.0 / p[i, i]
+            old = {a: p[key(a, i)] for a in range(8) if a != i}
+            fac = {a: old[a] * dinv_i for a in old}
+            for a in old:
+                for b in old:
+                    if a <= b:
+                        p[a, b] = p[a, b] - fac[a] * old[b]
+            for a in old:
+                p[key(a, i)] = fac[a]
+            p[i, i] = -dinv_i
+        return {(a, b): p[key(a, b)] for a in range(8) for b in range(8)}
+
+    for base in range(0, FSZ, BL):
+        r = [msc[pl.ds(base + i, 8, stride=FSZ), :] for i in range(BL)]
+        for lo in range(0, BL, 8):
+            at = base + lo
+            neg = invert8({
+                (a, b): at_lane(r[lo + a], at + b) for a in range(8) for b in range(a, 8)
+            })
+            inside = (lane8 >= at) & (lane8 < at + 8)
+            unit = [(lane8 == at + a).astype(F32) for a in range(8)]
+            plain = [jnp.where(inside, -unit[b], r[lo + b]) for b in range(8)]
+            y = []
+            for a in range(8):
+                acc = neg[a, 0] * plain[0]
+                for b in range(1, 8):
+                    acc += neg[a, b] * plain[b]
+                y.append(acc)
+            for i in range(lo + 8, BL):
+                acc = jnp.where(inside, 0.0, r[i])
+                for a in range(8):
+                    acc += at_lane(r[i], at + a) * y[a]
+                r[i] = acc
+            for a in range(8):
+                i = lo + a
+                wrow[8 * i : 8 * i + 8, :] = r[i] - unit[a]
+                zrow[8 * i : 8 * i + 8, :] = jnp.where(inside, unit[a], 0.0) - y[a]
+        two = jnp.where(laneb == rowb + base, 2.0, 0.0)
         for k in range(6):
-            xm = pltpu.roll(panels[k] - diag8, base, 1)
-            ym = pltpu.roll(jnp.where(lane8 < 8, diag8 - inv[k], inv[k]), base, 1)
-            x1, x2, x3 = split3(xm)
-            y1, y2, y3 = split3(ym)
-            xs = jnp.concatenate([x1, x1, x2, x2, x1, x3], axis=0).astype(BF16)
-            ys = jnp.concatenate([y1, y2, y1, y2, y3, y1], axis=0).astype(BF16)
+            xm = wrow[pl.ds(k, BL, stride=8), :]
+            ym = zrow[pl.ds(k, BL, stride=8), :]
+            x1 = xm.astype(BF16)
+            x2 = (xm - x1.astype(F32)).astype(BF16)
+            y1 = ym.astype(BF16)
+            y2 = (ym - y1.astype(F32)).astype(BF16)
+            xs = jnp.concatenate([x1, x1, x2], axis=0)
+            ys = jnp.concatenate([y1, y2, y1], axis=0)
             upd = lax.dot_general(xs, ys, (((0,), (0,)), ((), ())), preferred_element_type=F32)
-            msc[k] = msc[k] - upd
-            rows = jnp.where(lane8 < 8, -inv[k], inv[k])
-            msc[k, pl.ds(base, 8), :] = pltpu.roll(rows, base, 1)
-        return carry
-
-    lax.fori_loop(0, FSZ // 8, sweep, 0)
+            mat = slice(k * FSZ, (k + 1) * FSZ)
+            msc[mat, :] = msc[mat, :] - upd
+            own_rows = slice(k * FSZ + base, k * FSZ + base + BL)
+            msc[own_rows, :] = msc[own_rows, :] - two
+
     for k in range(6):
-        di = -(msc[k] * srows[k] * scols[k])
+        di = -(msc[k * FSZ : (k + 1) * FSZ, :] * srows[k] * scols[k])
         hi = di.astype(BF16)
         dinv[k, :, 0:FSZ] = hi
         dinv[k, :, FSZ:] = (di - hi.astype(F32)).astype(BF16)
@@ -457,8 +541,8 @@
     def _(o):
         axis_send(o).wait_send()
 
-    for o in order:
-        shard_to(o).wait_send()
+    for c in shards:
+        c.wait_send()
     tot = rb[0]
     for s in range(1, nz):
         tot = tot + rb[s]
@@ -504,13 +588,6 @@
 
 
 def per_device(nd, npl, elem_count, face_count, bound_slot, elem_face, density, coupling, ainv, loads):
-    odd = lax.rem(lax.axis_index("rhs"), 2) == 1
-    main = jnp.where(odd, coupling[:, :, 64:], coupling[:, :, :128])
-    mid = jnp.where(odd, coupling[:, :, :64], coupling[:, :, 128:])
-    a, b = mid[:, : TR // 2], mid[:, TR // 2 :]
-    mid = jnp.where(odd, jnp.concatenate([b, a], axis=2), jnp.concatenate([a, b], axis=2))
-    packed = jnp.concatenate([main, mid], axis=1)
-
     smem = pl.BlockSpec(memory_space=pltpu.SMEM)
     vmem = pl.BlockSpec(memory_space=pltpu.VMEM)
     hbm = pl.BlockSpec(memory_space=pl.ANY)
@@ -521,20 +598,25 @@
     return pl.pallas_call(
         functools.partial(kernel, nd, npl),
         out_shape=(out, out),
-        in_specs=[smem, smem, smem, smem, vmem, hbm, vmem, vmem],
+        in_specs=[smem, smem, smem, smem, vmem, hbm, vmem, hbm],
         out_specs=(vmem, vmem),
         scratch_shapes=[
+            vm((2, TR, 192), BF16),
+            vm((1152, FSZ), BF16),
+            vm((TR, TR), BF16),
             vm((4, 1152, FSZ), BF16),
             vm((TR, TR), BF16),
             vm((TR, TR), BF16),
             vm((TR, FSZ), F32),
             vm((8, TR), BF16),
             vm((NR, TR), F32),
-            vm((6, FSZ, FSZ), F32),
-            vm((6, FSZ, FSZ), F32),
-            vm((2, 2 * FSZ + 8, FSZ), F32),
-            vm((2, 2, 2 * FSZ + 8, FSZ), F32),
-            vm((6, FSZ, FSZ), F32),
+            vm((6, PK, FSZ), F32),
+            vm((6, PK, FSZ), F32),
+            vm((2, 2 * PK + 8, FSZ), F32),
+            vm((2, 2, 2 * PK + 8, FSZ), F32),
+            vm((8 * FSZ, FSZ), F32),
+            vm((8 * BL, FSZ), F32),
+            vm((8 * BL, FSZ), F32),
             vm((6, FSZ, 2 * FSZ), BF16),
             vm((4, NR, TR), F32),
             vm((4, 2, 2, NR, FSZ), F32),
@@ -548,7 +630,8 @@
             vm((2, 2, FSZ), F32),
             vm((2 * npl, 2, FSZ), F32),
             vm((nz, 2, FSZ), F32),
-            dma, dma((4,)), dma((4,)), dma, dma, dma((6,)), dma((6,)),
+            pltpu.SemaphoreType.REGULAR((2,)),
+            dma((3,)), dma((3,)), dma((4,)), dma, dma, dma((6,)), dma((6,)),
             dma((4, 5)), dma((4, 5)), dma((5,)), dma((5,)),
             dma((2 * npl,)), dma((2 * npl,)), dma((nz,)), dma((nz,)),
         ],
@@ -556,7 +639,7 @@
             collective_id=0, has_side_effects=True, vmem_limit_bytes=48 * 1024 * 1024
         ),
         name="condense_cg",
-    )(elem_count, face_count, bound_slot, elem_face, density, packed, loads, ainv)
+    )(elem_count, face_count, bound_slot, elem_face, density, coupling, loads, ainv)
 
 
 def solution(mesh):

time: 97 us -> 73.4 us (0.76)
  Pallas kernels: 90.3 us -> 68.5 us
  local copies, waits for them, and re-layouts: 4.04 us -> 2.59 us
    pallas_call x1, Pallas kernels: 90.3 us -> 68.5 us  [per_device(): pl.pallas_call(functools.partial(kernel, nd, npl), out_shape=(out, out),...]
    slice x3 -> x0, local copies, waits for them, and re-layouts: 1.14 us -> none  [the longest x1 1.06 us: per_device(): mid = jnp.where(odd, coupling[:, :, :64], coupling[:, :, 128:])]
    unnamed x18 -> x13, local copies, waits for them, and re-layouts: 2.9 us -> 2.59 us
where the time goes in v2:
time: 73.4 us; the launch traced here: 73.2 us
  Pallas kernels  68.5 us (93%)
  local copies, waits for them, and re-layouts  2.59 us (4%)
  between operations  2.11 us (3%)
    pallas_call x1, Pallas kernels, per_device(): pl.pallas_call(functools.partial(kernel, nd, npl), out_shape=(out, out),...  68.5 us
    unnamed x13, local copies, waits for them, and re-layouts  2.59 us

profile of v2, /device:TPU:1, one launch (start us, length us, event | category | flops | bytes accessed | tf_op | source)
XLA Modules:
  0.0 73.2 jit_solution(3672046045458778971)
XLA Ops:
  0.6 0.0 copy-start.1
  0.6 0.0 copy-start
  0.7 0.0 copy-start.2
  0.7 0.0 copy-start.3
  0.7 0.0 copy-start.4
  2.1 1.3 %copy.10.coup = bf16[2,768,192]{2,1,0:T(8,128)(2,1)S(1)} copy(bf16[2,768,192]{1,2,0:T(8,128)(2,1)} %param.13) | data formatting | bytes 1179648 | tf_op args[5]
  3.4 0.0 copy-done.1
  3.4 0.0 copy-done
  3.4 0.0 copy-done.2
  3.4 0.0 copy-done.3
  3.4 0.0 copy-done.4
  3.5 68.5 %condense_cg.1 = (f32[9,8,128]{2,1,0:T(8,128)S(1)}, f32[9,8,128]{2,1,0:T(8,128)S(1)}) custom-call(s32[1]{0:T(128)S(6)} %copy.13.ec, s32[1]{0:T(128)S(6)} %copy.14.fc, s32[1,2]{1,0:T(1,128)S(1)} %copy-done.4, s32[2,6]{1,0:T(2,128)S(1)} %copy-done.3, f32[2,768]{1,0:T(2,128)S(1)} %copy-done.2, bf16[2,768,192]{2,1,0:T(8,128)(2,1)S(1)} %copy.10.coup, ...), custom_call_target="tpu_custom_call" | custom-call | tf_op jit(solution)/shard_map/condense_cg/pallas_call | solution.py:598
  72.0 0.6 copy.15
  72.6 0.6 copy.16
Async XLA Ops:
  0.6 2.8 %copy-start.1 = (bf16[2,8,768]{2,1,0:T(8,128)(2,1)S(1)}, bf16[2,8,768]{2,1,0:T(8,128)(2,1)}, u32[]{:S(2)}) copy-start(bf16[2,8,768]{2,1,0:T(8,128)(2,1)} %loads.1) | copy-start | bytes 73732
  0.6 2.8 %copy-start = (bf16[768,768]{1,0:T(8,128)(2,1)S(1)}, bf16[768,768]{1,0:T(8,128)(2,1)}, u32[]{:S(2)}) copy-start(bf16[768,768]{1,0:T(8,128)(2,1)} %ainv.1) | copy-start | bytes 3538948
  0.7 2.8 %copy-start.2 = (f32[2,768]{1,0:T(2,128)S(1)}, f32[2,768]{1,0:T(2,128)}, u32[]{:S(2)}) copy-start(f32[2,768]{1,0:T(2,128)} %dens.1) | copy-start | bytes 18436
  0.7 2.8 %copy-start.3 = (s32[2,6]{1,0:T(2,128)S(1)}, s32[2,6]{1,0:T(2,128)}, u32[]{:S(2)}) copy-start(s32[2,6]{1,0:T(2,128)} %ef.1) | copy-start | bytes 148
  0.7 2.8 %copy-start.4 = (s32[1,2]{1,0:T(1,128)S(1)}, s32[1,2]{1,0:T(1,128)}, u32[]{:S(2)}) copy-start(s32[1,2]{1,0:T(1,128)} %bs.1) | copy-start | bytes 28

commit v3 on v2

--- a/solution.py
+++ b/solution.py
@@ -12,6 +12,7 @@
 TR = 768
 NR = 16
 PLANE = 8
+VMEM_ALL = 62 * 1024 * 1024
 PK = 72
 BL = 16
 F32 = jnp.float32
@@ -28,6 +29,10 @@
     return jnp.dot(a, b, preferred_element_type=F32)
 
 
+def mm_t(a, b):
+    return lax.dot_general(a, b, (((1,), (1,)), ((), ())), preferred_element_type=F32)
+
+
 def face(k):
     return slice(k * FSZ, (k + 1) * FSZ)
 
@@ -35,7 +40,7 @@
 def kernel(
     nd, npl,
     ec, fc, bs, ef, dens, coup, loads, ainv, sol, res,
-    cin, cpk, amt, craw, cmat, btm, sbc, lrecv, drv, dloc, dpar, dsnd, dnbr, msc, wrow, zrow, dinv,
+    amt, craw, cmat, btm, den, lown, lrecv, dloc, dpar, dsnd, dnbr, msc, wrow, zrow, dinv,
     tvec, tnb, rvec, rnb, vbuf, vpar, vnb, vnbr, outb, pay, ra, rb,
     near, lsem, csend, crecv, lsend, lrecvs, dsend, drecv, tsend, trecv, vsend, vrecv,
     asend, arecv, bsend, brecv,
@@ -54,10 +59,14 @@
     def dev(dd, xx):
         return {"dom": dd, "rhs": xx}
 
+    def rows_of(s):
+        return craw.at[pl.ds(pl.multiple_of(192 * s, 64), 192)]
+
     loc = [
-        pltpu.make_async_copy(coup.at[oe], cin.at[0], lsem.at[0]),
-        pltpu.make_async_copy(coup.at[e], cin.at[1], lsem.at[1]),
-        pltpu.make_async_copy(ainv, amt, lsem.at[2]),
+        pltpu.make_async_copy(dens, den, lsem.at[0]),
+        pltpu.make_async_copy(coup.at[e], rows_of(x), lsem.at[1]),
+        pltpu.make_async_copy(loads.at[e], lown, lsem.at[2]),
+        pltpu.make_async_copy(ainv, amt, lsem.at[3]),
     ]
     for c in loc:
         c.start()
@@ -72,6 +81,9 @@
     for q in range(2):
         hello(nxt, 2 * h + q)
         hello(prv, 2 * h + q)
+    beside = lax.rem(partner + 2, 4)
+    hello(nxt, beside)
+    hello(prv, beside)
 
     def plane_peer(o):
         s = lax.rem(me_a + o, 2 * npl)
@@ -90,30 +102,7 @@
     hello(above, x)
     hello(below, x)
 
-    odd = e
-    src = lax.broadcasted_iota(jnp.int32, (192, FSZ), 0)
-    dst = lax.broadcasted_iota(jnp.int32, (192, FSZ), 1)
-    first_mid = 128 * (1 - odd)
-
-    p_main = (src == dst + 64 * odd).astype(F32).astype(BF16)
-    is_mid = (src >= first_mid) & (src < first_mid + 64)
-    p_low = (is_mid & (src - first_mid == dst)).astype(F32)
-    p_high = (is_mid & (src - first_mid + 64 == dst)).astype(F32)
-    o32 = odd.astype(F32)
-    p_top = (p_low * (1.0 - o32) + p_high * o32).astype(BF16)
-    p_bot = (p_high * (1.0 - o32) + p_low * o32).astype(BF16)
-
-    def pack(raw, out):
-        out[0:TR, :] = mm(raw[...], p_main).astype(BF16)
-        mid = mm(raw[0 : TR // 2, :], p_top) + mm(raw[TR // 2 :, :], p_bot)
-        out[TR:, :] = mid.astype(BF16)
-
-    loc[0].wait()
-    pack(cin.at[0], cpk)
-    loc[1].wait()
-    pack(cin.at[1], craw.at[x])
-
-    pl.semaphore_wait(bar, 3 + 4 + 2 * npl - 1 + 2)
+    pl.semaphore_wait(bar, 3 + 6 + 2 * npl - 1 + 2)
 
     def remote(src, dst, ssem, rsem, dd, xx):
         return pltpu.make_async_remote_copy(
@@ -123,13 +112,13 @@
 
     far = lax.rem(x + 2, 4)
     shards = [
-        remote(cpk, craw.at[x], csend.at[0], crecv.at[x], d, partner),
-        remote(craw.at[x], craw.at[x], csend.at[2], crecv.at[x], d, far),
-        remote(cpk, craw.at[x], csend.at[1], crecv.at[x], d, lax.rem(partner + 2, 4)),
+        remote(coup.at[oe], rows_of(x), csend.at[0], crecv.at[x], d, partner),
+        remote(coup.at[e], rows_of(x), csend.at[2], crecv.at[x], d, far),
+        remote(coup.at[oe], rows_of(x), csend.at[1], crecv.at[x], d, beside),
     ]
 
     def shard_from(s):
-        return remote(cpk, craw.at[s], csend.at[0], crecv.at[s], d, partner)
+        return remote(coup.at[0], rows_of(s), csend.at[0], crecv.at[s], d, partner)
 
     for c in shards:
         c.start()
@@ -142,9 +131,8 @@
         pl.semaphore_wait(near.at[0], 1)
         pl.semaphore_wait(near.at[1], 1)
 
-    scal = lax.rsqrt(dens[pl.ds(e, 1), :])
-    for k in range(6):
-        sbc[face(k), :] = jnp.transpose(jnp.broadcast_to(scal[:, face(k)], (FSZ, FSZ)))
+    loc[0].wait()
+    scal = lax.rsqrt(den[pl.ds(e, 1), :])
 
     alive = (e < ec[0]).astype(F32)
     al = [(q < ec[0]).astype(F32) for q in range(2)]
@@ -169,10 +157,10 @@
         [eq(mine[k], NF + 1) * has_next, eq(mine[k], up_slot) * has_next] for k in range(6)
     ]
 
-    lane = lax.broadcasted_iota(jnp.int32, (TR // 2, FSZ), 1)
     row64 = lax.broadcasted_iota(jnp.int32, (64, FSZ), 0)
     lane64 = lax.broadcasted_iota(jnp.int32, (64, FSZ), 1)
-    loc[2].wait()
+    loc[1].wait()
+    loc[3].wait()
     amat = amt[...]
     for t in range(2):
         p = lax.rem(h + t, 2)
@@ -181,23 +169,14 @@
         else:
             shard_from(2 * p).wait_recv()
             shard_from(2 * p + 1).wait_recv()
-        cols = pl.multiple_of(p * 384, 128)
-        ev, od = craw.at[2 * p], craw.at[2 * p + 1]
-        cmat[:, pl.ds(cols, FSZ)] = (ev[0:TR, :].astype(F32) * sbc[...]).astype(BF16)
-        cmat[:, pl.ds(cols + 2 * FSZ, FSZ)] = (od[0:TR, :].astype(F32) * sbc[...]).astype(BF16)
-        m0, m1 = ev[TR:, :].astype(F32), od[TR:, :].astype(F32)
-        top = jnp.where(lane < 64, m0, m1)
-        bot = pltpu.roll(jnp.where(lane < 64, m1, m0), 64, 1)
-        half = TR // 2
-        cmat[0:half, pl.ds(cols + FSZ, FSZ)] = (top * sbc[0:half, :]).astype(BF16)
-        cmat[half:TR, pl.ds(cols + FSZ, FSZ)] = (bot * sbc[half:TR, :]).astype(BF16)
+        at = pl.multiple_of(p * 384, 128)
         for k in range(3):
-            ck = cmat[:, pl.ds(cols + k * FSZ, FSZ)]
-            bt = lax.dot_general(
-                ck, amat, (((0,), (0,)), ((), ())), preferred_element_type=F32
-            ).astype(BF16)
-            btm[pl.ds(cols + k * FSZ, FSZ), :] = bt
-            dk = mm(bt, ck) * (0.5 * alive)
+            rows = pl.ds(at + k * FSZ, FSZ)
+            ck = (craw[rows, :].astype(F32) * scal).astype(BF16)
+            cmat[rows, :] = ck
+            bt = mm(ck, amat).astype(BF16)
+            btm[rows, :] = bt
+            dk = mm_t(bt, ck) * (0.5 * alive)
             dk = dk + jnp.transpose(dk)
             lower = pltpu.roll(dk[64:, :], 64, 1)
             dloc[3 * p + k, 0:64, :] = jnp.where((lane64 < 64) & (lane64 < row64), lower, dk[:64, :])
@@ -209,8 +188,6 @@
         remote(dloc.at[0:3], dpar.at[0:3], dsend.at[0], drecv.at[0], d, xl),
         remote(dloc.at[3:6], dpar.at[3:6], dsend.at[1], drecv.at[1], d, xr),
     ]
-    for c in dcp:
-        c.start()
     for side, table in enumerate((to_next, to_prev)):
         for s in range(2):
             acc = table[s][0] * dloc[0]
@@ -221,18 +198,19 @@
         live = (slot < fc[0]).astype(F32)
         dsnd[side, 2 * PK :, :] = jnp.full((8, FSZ), 1.0, F32) * live
     for side, dd in enumerate((nxt, prv)):
-        for q in range(2):
+        for q, xx in enumerate((x, (partner, beside)[side])):
             c = remote(
                 dsnd.at[side], dnbr.at[side, e], dsend.at[2 + 2 * side + q],
-                drecv.at[2 + 2 * side + e], dd, 2 * h + q,
+                drecv.at[2 + 2 * side + e], dd, xx,
             )
-            c.start()
             dcp.append(c)
+
+    for c in dcp[2:] + dcp[:2]:
+        c.start()
 
     def send_all(ex, t):
         tvec[ex] = t
         out = [remote(tvec.at[ex], rvec.at[ex], tsend.at[ex, 0], trecv.at[ex, 0], d, partner)]
-        out[0].start()
         for side, table in enumerate((to_next, to_prev)):
             for s in range(2):
                 acc = table[s][0] * t[:, face(0)]
@@ -247,9 +225,10 @@
                 )
                 c.start()
                 out.append(c)
+        out[0].start()
         return out
 
-    def assemble(ex, t, cps):
+    def settle(ex, cps):
         for c in cps:
             c.wait_send()
         remote(tvec.at[ex], rvec.at[ex], tsend.at[ex, 0], trecv.at[ex, 0], d, partner).wait_recv()
@@ -259,6 +238,9 @@
                     tnb.at[ex, side], rnb.at[ex, side, q], tsend.at[ex, 0],
                     trecv.at[ex, 1 + 2 * side + q], d, partner,
                 ).wait_recv()
+
+    def assemble(ex, t, cps):
+        settle(ex, cps)
         pv = [rnb[ex, 0, 0, s] + rnb[ex, 0, 1, s] for s in range(2)]
         nv = [rnb[ex, 1, 0, s] + rnb[ex, 1, 1, s] for s in range(2)]
         other = [rvec[ex, :, face(q)] for q in range(6)]
@@ -273,9 +255,10 @@
         return jnp.concatenate(cols, axis=1)
 
     lcopy.wait()
+    loc[2].wait()
     srow = scal
     wgt = [
-        (loads[e].astype(F32) * srow).astype(BF16).astype(F32),
+        (lown[...].astype(F32) * srow).astype(BF16).astype(F32),
         (lrecv[...].astype(F32) * srow).astype(BF16).astype(F32),
     ]
     low = e == 0
@@ -283,8 +266,7 @@
         [jnp.where(low, wgt[0], wgt[1]), jnp.where(low, wgt[1], wgt[0])], axis=0
     ).astype(BF16)
     forced = mm(weighted, amat).astype(BF16)
-    rloc = mm(forced, cmat[...]) * alive
-    drv[...] = rloc
+    rloc = mm_t(forced, cmat[...]) * alive
     rcp = send_all(0, rloc)
 
     for c in dcp:
@@ -413,21 +395,47 @@
     def apply_s(v):
         u = mm(parts(v), btm[...])
         u = u[:NR] + u[NR:]
-        t = mm(parts(u), cmat[...])
+        t = mm_t(parts(u), cmat[...])
         return (t[:NR] + t[NR:]) * alive
 
-    r0 = assemble(0, rloc, rcp)
-    vbuf[3] = r0
-    w = precondition(r0)
-    vbuf[0] = w
+    m0 = [sum(eq(n0[k], f) for k in range(6)) * al[0] for f in range(NF + 2)]
+    m1 = [sum(eq(n1[k], f) for k in range(6)) * al[1] for f in range(NF + 2)]
+    mine_w = [jnp.where(e == 0, al[0], al[1] * (1.0 - m0[f])) for f in range(NF + 2)]
+    their_w = [jnp.where(e == 1, al[0], al[1] * (1.0 - m0[f])) for f in range(NF + 2)]
+
+    def hand_on(v, w):
+        vbuf[v] = w
+        out = [
+            remote(
+                vbuf.at[v, pl.ds(pl.multiple_of(8 * oe, 8), 8), :], vpar.at[v], vsend.at[v, 0],
+                vrecv.at[v, 0], d, partner,
+            )
+        ]
+        for side, name in enumerate((NF + 1, NF)):
+            acc = jnp.zeros((NR, FSZ), F32)
+            for k in range(6):
+                acc += (eq(mine[k], name) * mine_w[name]) * w[:, face(k)]
+            vnb[side, v] = acc
+            for q in range(2):
+                out.append(
+                    remote(
+                        vnb.at[side, v, 8 * q : 8 * q + 8, :], vnbr.at[side, e, v],
+                        vsend.at[v, 1 + 2 * side + q], vrecv.at[v, 1 + 2 * side + e],
+                        (nxt, prv)[side], 2 * h + q,
+                    )
+                )
+        for c in out:
+            c.start()
+        return out
+
+    w = precondition(assemble(0, rloc, rcp))
+    vcp = []
     for i in range(3):
         t = apply_s(w)
         cps = send_all(1 + i, t)
+        vcp += hand_on(i, w)
         if i < 2:
-            full = assemble(1 + i, t, cps)
-            vbuf[4 + i] = full
-            w = precondition(full) - w
-            vbuf[1 + i] = w
+            w = precondition(assemble(1 + i, t, cps)) - w
 
     def fold(v):
         acc = v[:, face(0)]
@@ -440,7 +448,7 @@
         wi = vbuf[i]
         for j in range(3):
             prods.append(fold(wi * tvec[1 + j]))
-        prods.append(fold(wi * drv[...]))
+        prods.append(fold(wi * tvec[0]))
     pads = [jnp.zeros((NR, FSZ), F32)] * 4
     for c in range(2):
         stack = jnp.concatenate((prods + pads)[8 * c : 8 * c + 8], axis=0)
@@ -481,53 +489,37 @@
     def _(o):
         axis_send(o).start()
 
-    vbuf[6] = assemble(3, t, cps)
-    m0 = [sum(eq(n0[k], f) for k in range(6)) * al[0] for f in range(NF + 2)]
-    m1 = [sum(eq(n1[k], f) for k in range(6)) * al[1] for f in range(NF + 2)]
-    mine_w = [jnp.where(e == 0, al[0], al[1] * (1.0 - m0[f])) for f in range(NF + 2)]
-    their_w = [jnp.where(e == 1, al[0], al[1] * (1.0 - m0[f])) for f in range(NF + 2)]
-    for side, name in enumerate((NF + 1, NF)):
-        for v in range(7):
-            acc = jnp.zeros((NR, FSZ), F32)
-            for k in range(6):
-                acc += (eq(mine[k], name) * mine_w[name]) * vbuf[v, :, face(k)]
-            vnb[side, v] = acc
-    vcp = [
-        remote(
-            vbuf.at[:, pl.ds(pl.multiple_of(8 * oe, 8), 8), :], vpar, vsend.at[0], vrecv.at[0],
-            d, partner,
-        )
-    ]
-    for side, dd in enumerate((nxt, prv)):
-        for q in range(2):
-            vcp.append(
-                remote(
-                    vnb.at[side, :, 8 * q : 8 * q + 8, :], vnbr.at[side, e],
-                    vsend.at[1 + 2 * side + q], vrecv.at[1 + 2 * side + e], dd, 2 * h + q,
-                )
-            )
-    for c in vcp:
-        c.start()
+    settle(3, cps)
     for c in vcp:
         c.wait_send()
-    remote(vpar, vpar, vsend.at[0], vrecv.at[0], d, partner).wait_recv()
-    for side in range(2):
-        for q in range(2):
-            remote(
-                vnb.at[side, :, 0:8, :], vnbr.at[side, q], vsend.at[0],
-                vrecv.at[1 + 2 * side + q], d, partner,
-            ).wait_recv()
+    for v in range(3):
+        remote(vpar.at[v], vpar.at[v], vsend.at[0, 0], vrecv.at[v, 0], d, partner).wait_recv()
+        for side in range(2):
+            for q in range(2):
+                remote(
+                    vnb.at[side, v, 0:8, :], vnbr.at[side, q, v], vsend.at[0, 0],
+                    vrecv.at[v, 1 + 2 * side + q], d, partner,
+                ).wait_recv()
     rows = pl.ds(pl.multiple_of(8 * e, 8), 8)
     for f in range(NF):
         free = 1.0 - jnp.maximum(m0[f], m1[f])
         wp = free * eq(lo_slot, f) * has_prev
         wn = free * eq(up_slot, f) * has_next
-        for v in range(7):
+        for v in range(3):
             acc = wp * (vnbr[0, 0, v] + vnbr[0, 1, v]) + wn * (vnbr[1, 0, v] + vnbr[1, 1, v])
             for k in range(6):
                 acc += (eq(mine[k], f) * mine_w[f]) * vbuf[v, rows, face(k)]
                 acc += (eq(theirs[k], f) * their_w[f]) * vpar[v, :, face(k)]
             outb[v, f] = acc
+        tp = eq(lo_slot, f) * has_prev
+        tn = eq(up_slot, f) * has_next
+        for ex in range(4):
+            acc = tp * (rnb[ex, 0, 0, 1, rows, :] + rnb[ex, 0, 1, 1, rows, :])
+            acc += tn * (rnb[ex, 1, 0, 1, rows, :] + rnb[ex, 1, 1, 1, rows, :])
+            for k in range(6):
+                acc += eq(mine[k], f) * tvec[ex, rows, face(k)]
+                acc += eq(theirs[k], f) * rvec[ex, rows, face(k)]
+            outb[3 + ex, f] = acc
 
     @pl.loop(1, 2 * npl)
     def _(o):
@@ -588,28 +580,27 @@
 
 
 def per_device(nd, npl, elem_count, face_count, bound_slot, elem_face, density, coupling, ainv, loads):
+    columns = jnp.swapaxes(coupling, 1, 2)
     smem = pl.BlockSpec(memory_space=pltpu.SMEM)
     vmem = pl.BlockSpec(memory_space=pltpu.VMEM)
-    hbm = pl.BlockSpec(memory_space=pl.ANY)
+    hbm = pl.BlockSpec(memory_space=pltpu.HBM)
     dma = pltpu.SemaphoreType.DMA
     nz = nd // npl
-    out = jax.ShapeDtypeStruct((NF, 8, FSZ), F32)
+    out = pltpu.VMEM((NF, 8, FSZ), F32)
     vm = pltpu.VMEM
     return pl.pallas_call(
         functools.partial(kernel, nd, npl),
         out_shape=(out, out),
-        in_specs=[smem, smem, smem, smem, vmem, hbm, vmem, hbm],
+        in_specs=[smem, smem, smem, smem, hbm, hbm, hbm, hbm],
         out_specs=(vmem, vmem),
         scratch_shapes=[
-            vm((2, TR, 192), BF16),
-            vm((1152, FSZ), BF16),
-            vm((TR, TR), BF16),
-            vm((4, 1152, FSZ), BF16),
             vm((TR, TR), BF16),
             vm((TR, TR), BF16),
-            vm((TR, FSZ), F32),
+            vm((TR, TR), BF16),
+            vm((TR, TR), BF16),
+            vm((2, TR), F32),
             vm((8, TR), BF16),
-            vm((NR, TR), F32),
+            vm((8, TR), BF16),
             vm((6, PK, FSZ), F32),
             vm((6, PK, FSZ), F32),
             vm((2, 2 * PK + 8, FSZ), F32),
@@ -622,24 +613,24 @@
             vm((4, 2, 2, NR, FSZ), F32),
             vm((4, NR, TR), F32),
             vm((4, 2, 2, 2, NR, FSZ), F32),
-            vm((7, NR, TR), F32),
-            vm((7, 8, TR), F32),
-            vm((2, 7, NR, FSZ), F32),
-            vm((2, 2, 7, 8, FSZ), F32),
+            vm((3, NR, TR), F32),
+            vm((3, 8, TR), F32),
+            vm((2, 3, NR, FSZ), F32),
+            vm((2, 2, 3, 8, FSZ), F32),
             vm((7, NF, 8, FSZ), F32),
             vm((2, 2, FSZ), F32),
             vm((2 * npl, 2, FSZ), F32),
             vm((nz, 2, FSZ), F32),
             pltpu.SemaphoreType.REGULAR((2,)),
-            dma((3,)), dma((3,)), dma((4,)), dma, dma, dma((6,)), dma((6,)),
-            dma((4, 5)), dma((4, 5)), dma((5,)), dma((5,)),
+            dma((4,)), dma((3,)), dma((4,)), dma, dma, dma((6,)), dma((6,)),
+            dma((4, 5)), dma((4, 5)), dma((3, 5)), dma((3, 5)),
             dma((2 * npl,)), dma((2 * npl,)), dma((nz,)), dma((nz,)),
         ],
         compiler_params=pltpu.CompilerParams(
-            collective_id=0, has_side_effects=True, vmem_limit_bytes=48 * 1024 * 1024
+            collective_id=0, has_side_effects=True, vmem_limit_bytes=VMEM_ALL
         ),
         name="condense_cg",
-    )(elem_count, face_count, bound_slot, elem_face, density, coupling, loads, ainv)
+    )(elem_count, face_count, bound_slot, elem_face, density, columns, loads, ainv)
 
 
 def solution(mesh):

time: 73.4 us -> 71.7 us (0.977)
  local copies, waits for them, and re-layouts: 2.59 us -> 1.23 us
    unnamed x13 -> x2, local copies, waits for them, and re-layouts: 2.59 us -> 1.23 us
where the time goes in v3:
time: 71.7 us; the launch traced here: 71.6 us
  Pallas kernels  68.4 us (95%)
  between operations  1.93 us (3%)
  local copies, waits for them, and re-layouts  1.23 us (2%)
    pallas_call x1, Pallas kernels, per_device(): pl.pallas_call(functools.partial(kernel, nd, npl), out_shape=(out, out),...  68.4 us

profile of v3, /device:TPU:1, one launch (start us, length us, event | category | flops | bytes accessed | tf_op | source)
XLA Modules:
  0.0 71.6 jit_solution(13866806695230270798)
XLA Ops:
  1.9 68.4 %condense_cg.1 = (f32[9,8,128]{2,1,0:T(8,128)S(1)}, f32[9,8,128]{2,1,0:T(8,128)S(1)}) custom-call(s32[1]{0:T(128)S(6)} %copy.14.ec, s32[1]{0:T(128)S(6)} %copy.15.fc, s32[1,2]{1,0:T(1,128)} %bs.1, s32[2,6]{1,0:T(2,128)} %ef.1, f32[2,768]{1,0:T(2,128)} %dens.1, bf16[2,192,768]{2,1,0:T(8,128)(2,1)} %bitcast.1, bf16[2,8,768]{2,1,0:T(8,128)(2,1)} %loads.1, ...), custom_call_target="tpu_custom_call" | custom-call | tf_op jit(solution)/shard_map/condense_cg/pallas_call | solution.py:591
  70.3 0.6 copy.12
  70.9 0.6 copy.13

commit v4 on v3

--- a/solution.py
+++ b/solution.py
@@ -39,8 +39,8 @@
 
 def kernel(
     nd, npl,
-    ec, fc, bs, ef, dens, coup, loads, ainv, sol, res,
-    amt, craw, cmat, btm, den, lown, lrecv, dloc, dpar, dsnd, dnbr, msc, wrow, zrow, dinv,
+    ec, fc, bs_in, ef_in, dens, coup, loads, ainv, sol, res,
+    bs, ef, amt, craw, cmat, btm, den, lown, lrecv, dloc, dpar, dsnd, dnbr, msc, wrow, zrow, dinv,
     tvec, tnb, rvec, rnb, vbuf, vpar, vnb, vnbr, outb, pay, ra, rb,
     near, lsem, csend, crecv, lsend, lrecvs, dsend, drecv, tsend, trecv, vsend, vrecv,
     asend, arecv, bsend, brecv,
@@ -67,9 +67,9 @@
         pltpu.make_async_copy(coup.at[e], rows_of(x), lsem.at[1]),
         pltpu.make_async_copy(loads.at[e], lown, lsem.at[2]),
         pltpu.make_async_copy(ainv, amt, lsem.at[3]),
+        pltpu.make_async_copy(bs_in, bs, lsem.at[4]),
+        pltpu.make_async_copy(ef_in, ef, lsem.at[5]),
     ]
-    for c in loc:
-        c.start()
 
     bar = pltpu.get_barrier_semaphore()
 
@@ -102,6 +102,8 @@
     hello(above, x)
     hello(below, x)
 
+    for c in loc:
+        c.start()
     pl.semaphore_wait(bar, 3 + 6 + 2 * npl - 1 + 2)
 
     def remote(src, dst, ssem, rsem, dd, xx):
@@ -134,6 +136,8 @@
     loc[0].wait()
     scal = lax.rsqrt(den[pl.ds(e, 1), :])
 
+    for c in loc[4:]:
+        c.wait()
     alive = (e < ec[0]).astype(F32)
     al = [(q < ec[0]).astype(F32) for q in range(2)]
     n0 = [ef[0, k] for k in range(6)]
@@ -431,9 +435,9 @@
     w = precondition(assemble(0, rloc, rcp))
     vcp = []
     for i in range(3):
+        vcp += hand_on(i, w)
         t = apply_s(w)
         cps = send_all(1 + i, t)
-        vcp += hand_on(i, w)
         if i < 2:
             w = precondition(assemble(1 + i, t, cps)) - w
 
@@ -591,9 +595,11 @@
     return pl.pallas_call(
         functools.partial(kernel, nd, npl),
         out_shape=(out, out),
-        in_specs=[smem, smem, smem, smem, hbm, hbm, hbm, hbm],
+        in_specs=[smem, smem] + [hbm] * 6,
         out_specs=(vmem, vmem),
         scratch_shapes=[
+            pltpu.SMEM((1, 2), jnp.int32),
+            pltpu.SMEM((2, 6), jnp.int32),
             vm((TR, TR), BF16),
             vm((TR, TR), BF16),
             vm((TR, TR), BF16),
@@ -622,7 +628,7 @@
             vm((2 * npl, 2, FSZ), F32),
             vm((nz, 2, FSZ), F32),
             pltpu.SemaphoreType.REGULAR((2,)),
-            dma((4,)), dma((3,)), dma((4,)), dma, dma, dma((6,)), dma((6,)),
+            dma((6,)), dma((3,)), dma((4,)), dma, dma, dma((6,)), dma((6,)),
             dma((4, 5)), dma((4, 5)), dma((3, 5)), dma((3, 5)),
             dma((2 * npl,)), dma((2 * npl,)), dma((nz,)), dma((nz,)),
         ],

time: 71.7 us -> 71 us (level)
  no operation moved by 1% of the time
where the time goes in v4:
time: 71 us; the launch traced here: 70.9 us
  Pallas kernels  67.7 us (95%)
  between operations  1.93 us (3%)
  local copies, waits for them, and re-layouts  1.23 us (2%)
    pallas_call x1, Pallas kernels, per_device(): pl.pallas_call(functools.partial(kernel, nd, npl), out_shape=(out, out),...  67.7 us

profile of v4, /device:TPU:1, one launch (start us, length us, event | category | flops | bytes accessed | tf_op | source)
XLA Modules:
  0.0 70.9 jit_solution(5004403921747927158)
XLA Ops:
  1.9 67.7 %condense_cg.1 = (f32[9,8,128]{2,1,0:T(8,128)S(1)}, f32[9,8,128]{2,1,0:T(8,128)S(1)}) custom-call(s32[1]{0:T(128)S(6)} %copy.14.ec, s32[1]{0:T(128)S(6)} %copy.15.fc, s32[1,2]{1,0:T(1,128)} %bs_in.1, s32[2,6]{1,0:T(2,128)} %ef_in.1, f32[2,768]{1,0:T(2,128)} %dens.1, bf16[2,192,768]{2,1,0:T(8,128)(2,1)} %bitcast.1, bf16[2,8,768]{2,1,0:T(8,128)(2,1)} %loads.1, ...), custom_call_target="tpu_custom_call" | custom-call | tf_op jit(solution)/shard_map/condense_cg/pallas_call | solution.py:595
  69.7 0.6 copy.12
  70.3 0.6 copy.13

commit v5 on v4

--- a/solution.py
+++ b/solution.py
@@ -212,6 +212,8 @@
     for c in dcp[2:] + dcp[:2]:
         c.start()
 
+    sent = []
+
     def send_all(ex, t):
         tvec[ex] = t
         out = [remote(tvec.at[ex], rvec.at[ex], tsend.at[ex, 0], trecv.at[ex, 0], d, partner)]
@@ -233,8 +235,7 @@
         return out
 
     def settle(ex, cps):
-        for c in cps:
-            c.wait_send()
+        sent.extend(cps)
         remote(tvec.at[ex], rvec.at[ex], tsend.at[ex, 0], trecv.at[ex, 0], d, partner).wait_recv()
         for side in range(2):
             for q in range(2):
@@ -273,8 +274,7 @@
     rloc = mm_t(forced, cmat[...]) * alive
     rcp = send_all(0, rloc)
 
-    for c in dcp:
-        c.wait_send()
+    sent.extend(dcp)
     remote(dloc.at[0:3], dpar.at[0:3], dsend.at[0], drecv.at[0], d, partner).wait_recv()
     remote(dloc.at[3:6], dpar.at[3:6], dsend.at[0], drecv.at[1], d, partner).wait_recv()
     for side in range(2):
@@ -494,8 +494,7 @@
         axis_send(o).start()
 
     settle(3, cps)
-    for c in vcp:
-        c.wait_send()
+    sent.extend(vcp)
     for v in range(3):
         remote(vpar.at[v], vpar.at[v], vsend.at[0, 0], vrecv.at[v, 0], d, partner).wait_recv()
         for side in range(2):
@@ -537,7 +536,7 @@
     def _(o):
         axis_send(o).wait_send()
 
-    for c in shards:
+    for c in shards + sent:
         c.wait_send()
     tot = rb[0]
     for s in range(1, nz):

time: 71 us -> 71.1 us (level)
  no operation moved by 1% of the time
where the time goes in v5:
time: 71.1 us; the launch traced here: 70.9 us
  Pallas kernels  67.8 us (95%)
  between operations  1.93 us (3%)
  local copies, waits for them, and re-layouts  1.23 us (2%)
    pallas_call x1, Pallas kernels, per_device(): pl.pallas_call(functools.partial(kernel, nd, npl), out_shape=(out, out),...  67.8 us

profile of v5, /device:TPU:1, one launch (start us, length us, event | category | flops | bytes accessed | tf_op | source)
XLA Modules:
  0.0 70.9 jit_solution(17911460128037903320)
XLA Ops:
  1.9 67.8 %condense_cg.1 = (f32[9,8,128]{2,1,0:T(8,128)S(1)}, f32[9,8,128]{2,1,0:T(8,128)S(1)}) custom-call(s32[1]{0:T(128)S(6)} %copy.14.ec, s32[1]{0:T(128)S(6)} %copy.15.fc, s32[1,2]{1,0:T(1,128)} %bs_in.1, s32[2,6]{1,0:T(2,128)} %ef_in.1, f32[2,768]{1,0:T(2,128)} %dens.1, bf16[2,192,768]{2,1,0:T(8,128)(2,1)} %bitcast.1, bf16[2,8,768]{2,1,0:T(8,128)(2,1)} %loads.1, ...), custom_call_target="tpu_custom_call" | custom-call | tf_op jit(solution)/shard_map/condense_cg/pallas_call | solution.py:594
  69.7 0.6 copy.12
  70.3 0.6 copy.13
